TPU v7x, 32 devices: a whole 2x2x4 slice. The times are simulated.
32 devices in a mesh: section: 2 (over y), blk: 8 (over z, x), mp: 2 (over core).
Axes of the slice: x: 2, y: 2, z: 4, core: 2. Of those that a mesh axis runs over, the one named last changes fastest.
Arguments:
- queries: bfloat16 [2, 1024, 4096], P('section', 'blk', 'mp'), may hold values from -210 to 210
- encoder_states: bfloat16 [512, 2048], P(('blk', 'section', 'mp')), may hold values from -200 to 200
- norm_gain: float32 [2048], replicated, may hold values from 0.25 to 1.75
- kv_weight: bfloat16 [2, 2048, 2, 512], P('section', 'blk', None, 'mp'), may hold values from -0.125 to 0.125
- span_len: int32 [64], replicated, may hold values from 1 to 57, as said below
- span_owner: int32 [64], replicated, may hold values from 0 to 7, as said below
Outputs:
- attended: bfloat16 [2, 1024, 4096], P('section', 'blk', 'mp')
Inputs may be any that keep to these rules, and one draw needn't show every extreme that they name: `span_owner`: each span lies whole in the slots of one blk index; each blk index owns exactly 8 spans. `span_len`: the spans of one blk index hold at most 64 tokens together, exactly 64 for some blk index in every draw; all spans hold 288 tokens together; one span holds exactly 57 tokens in every draw.
All inputs are finite; a program needn't handle non-finite values.
Results may differ from a plain program's by a relative error of at most 0.0094.
Values may be sent and summed in bfloat16 or wider, within the bound.
No kernel may reach another device: no remote copies, remote signals or barrier semaphores. Data moves between devices by JAX's collectives and lax.ppermute only.
A program may use at most 64 MiB of HBM per device.

v0:
```python
import jax
import jax.numpy as jnp
from jax import lax
from jax.sharding import PartitionSpec as P

HEADS = 32
KVH = 4
HD = 128


def normalize(states, norm_gain):
    widened = states.astype(jnp.float32)
    factor = lax.rsqrt(jnp.mean(widened * widened, axis=-1, keepdims=True) + 1e-05)
    return (widened * factor * norm_gain).astype(jnp.bfloat16)


def slot_loads(span_len, span_owner, block_count):
    owners = span_owner[:, None] == jnp.arange(block_count, dtype=jnp.int32)[None, :]
    return jnp.sum(jnp.where(owners, span_len[:, None], 0), axis=0)


def live_slots(slot_load, row_count, capacity):
    slot_ids = jnp.arange(row_count, dtype=jnp.int32)
    holder = slot_ids // capacity
    picked = holder[:, None] == jnp.arange(slot_load.shape[0], dtype=jnp.int32)[None, :]
    holder_load = jnp.sum(jnp.where(picked, slot_load[None, :], 0), axis=1)
    return slot_ids % capacity < holder_load


def attend_block(state_now, query_grid, key_rows, value_rows, alive):
    running_max, denominator, numerator = state_now
    row_count = key_rows.shape[0]
    groups = query_grid.shape[1]
    head_size = query_grid.shape[3]
    key_grid = key_rows.reshape(row_count, groups, head_size)
    value_grid = value_rows.reshape(row_count, groups, head_size)
    scores = jnp.einsum(
        "qgjd,rgd->qgjr", query_grid, key_grid, preferred_element_type=jnp.float32
    ) * head_size ** (-0.5)
    scores = jnp.where(alive, scores, -1e30)
    new_max = jnp.maximum(running_max, jnp.max(scores, axis=-1))
    weights = jnp.where(alive, jnp.exp(scores - new_max[..., None]), 0.0)
    denominator = jnp.sum(weights, axis=-1)
    numerator = jnp.einsum(
        "qgjr,rgd->qgjd",
        weights.astype(jnp.bfloat16),
        value_grid,
        preferred_element_type=jnp.float32,
    )
    return (new_max, denominator, numerator)


def attend(state_now, query_grid, key_rows, value_rows, slot_load, capacity):
    row_count = key_rows.shape[0]
    alive = live_slots(slot_load, row_count, capacity)
    return attend_block(state_now, query_grid, key_rows, value_rows, alive)


def local(queries, encoder_states, norm_gain, kv_weight, span_len, span_owner):
    gathered = lax.all_gather(encoder_states, ("section", "mp"), axis=0, tiled=True)
    capacity = gathered.shape[0]
    normed = normalize(gathered, norm_gain)
    block_count = lax.axis_size("blk")
    slot_load = slot_loads(span_len, span_owner, block_count)
    group_width = kv_weight.shape[3]
    local_groups = group_width // HD
    group_size = HEADS // KVH
    query_rows = queries.shape[1]
    query_grid = queries[0].reshape(query_rows, local_groups, group_size, HD)
    start_state = (
        jnp.full((query_rows, local_groups, group_size), -1e30, jnp.float32),
        jnp.zeros((query_rows, local_groups, group_size), jnp.float32),
        jnp.zeros((query_rows, local_groups, group_size, HD), jnp.float32),
    )
    projected = jnp.einsum(
        "cr,rtk->ctk",
        normed,
        lax.all_gather(kv_weight, "blk", axis=1, tiled=True)[0],
        preferred_element_type=jnp.float32,
    )
    key_rows = projected[:, 0].astype(jnp.bfloat16)
    value_rows = projected[:, 1].astype(jnp.bfloat16)
    final_state = attend(
        start_state,
        query_grid,
        lax.all_gather(key_rows, "blk", axis=0, tiled=True),
        lax.all_gather(value_rows, "blk", axis=0, tiled=True),
        slot_load,
        capacity,
    )
    denominator = final_state[1]
    numerator = final_state[2]
    attended = (numerator / denominator[..., None]).astype(jnp.bfloat16)
    return attended.reshape(1, query_rows, local_groups * group_size * HD)


def solution(mesh):
    in_specs = (
        P("section", "blk", "mp"),
        P(("blk", "section", "mp"), None),
        P(),
        P("section", "blk", None, "mp"),
        P(),
        P(),
    )
    out_specs = P("section", "blk", "mp")
    return jax.shard_map(local, mesh=mesh, in_specs=in_specs, out_specs=out_specs, check_vma=False)
```

profile of v0, /device:TPU:0, one launch (start us, length us, event | category | flops | bytes accessed | tf_op | source)
XLA Modules:
  0.0 140.6 jit_solution(526181429607966376)
XLA Ops:
  6.5 0.0 all-gather.4.cloned.1.call-start
  6.5 1.7 %copy.13 = bf16[1,256,2,256]{3,1,2,0:T(8,128)(2,1)} copy(bf16[1,256,2,256]{3,2,1,0:T(2,128)(2,1)} %param.9) | data formatting | bytes 524288 | tf_op args[3]
  8.2 0.0 all-gather.4.cloned.1.call-update
  8.2 1.1 copy.25
  9.4 7.5 %all_gather.12 = bf16[64,2048]{1,0:T(8,128)(2,1)S(1)} all-gather(bf16[16,2048]{1,0:T(8,128)(2,1)} %param.7), channel_id=1, replica_groups=mesh['section'=2,'blk'=8,'mp'=2] {'section','mp'}, dimensions={0}, use_global_device_ids=true | all-gather | bytes 327680 | tf_op jit(solution)/shard_map/all_gather | solution.py:60
  16.9 0.8 select_reduce_fusion.1
  17.6 0.1 select_reduce_fusion
  17.7 0.2 fusion.18
  17.9 43.4 %all-gather.4.cloned.1.call-done = bf16[1,2048,2,256]{3,1,2,0:T(8,128)(2,1)} async-done(((bf16[1,256,2,256]{3,1,2,0:T(8,128)(2,1)}), bf16[1,2048,2,256]{3,1,2,0:T(8,128)(2,1)}) %all-gather.4.cloned.1.call-update) | async-done | bytes 2097168 | tf_op jit(solution)/shard_map/all_gather | solution.py:78
  61.3 2.1 %fusion.13 = bf16[64,2,256]{2,0,1:T(8,128)(2,1)S(1)} fusion(bf16[1,2048,2,256]{3,1,2,0:T(8,128)(2,1)} %all-gather.4.cloned.1.call-done, bf16[64,2048]{1,0:T(8,128)(2,1)S(1)} %all_gather.12, f32[2048]{0:T(1024)} %param.8, f32[64]{0:T(128)S(1)} %add_rsqrt_fusion), kind=kOutput, calls=%fused_computation.13 | convolution fusion | flops 134774784 | bytes 2433280 | tf_op jit(solution)/shard_map/cr,rtk->ctk/dot_general | solution.py:75
  63.5 30.8 %all-gather.1 = bf16[512,1,256]{2,0,1:T(8,128)(2,1)S(1)} all-gather(bf16[64,1,256]{2,0,1:T(8,128)(2,1)S(1)} %get-tuple-element.5), channel_id=3, replica_groups=mesh['section'=2,'blk'=8,'mp'=2] {'blk'}, dimensions={0}, use_global_device_ids=true | all-gather | bytes 294912 | tf_op jit(solution)/shard_map/all_gather | solution.py:86
  94.3 0.1 reshape.41
  94.4 2.7 %bitcast_reduce_fusion = (f32[128,2,8]{0,2,1:T(8,128)S(1)}, f32[2,512,128,8]{2,1,3,0:T(8,128)}) fusion(pred[512]{0:T(512)(128)(4,1)S(1)} %fusion.28, bf16[128,2,8,128]{3,2,1,0:T(8,128)(2,1)S(1)} %bitcast.42, bf16[512,2,128,1]{2,1,0,3:T(2,128)(2,1)S(1)} %bitcast.43), kind=kOutput, calls=%fused_computation.1 | convolution fusion | flops 271579136 | bytes 4989440 | tf_op jit(solution)/shard_map/qgjd,rgd->qgjr/dot_general | solution.py:37
  97.1 30.8 %all-gather = bf16[512,1,256]{2,0,1:T(8,128)(2,1)S(1)} all-gather(bf16[64,1,256]{2,0,1:T(8,128)(2,1)S(1)} %get-tuple-element.6), channel_id=2, replica_groups=mesh['section'=2,'blk'=8,'mp'=2] {'blk'}, dimensions={0}, use_global_device_ids=true | all-gather | bytes 294912 | tf_op jit(solution)/shard_map/all_gather | solution.py:87
  127.9 0.1 copy.22
  128.0 0.0 copy-start
  128.0 3.4 %fusion.2 = f32[128,2,8]{0,2,1:T(8,128)S(1)} fusion(f32[2,512,128,8]{2,1,3,0:T(8,128)} %get-tuple-element.8, f32[128,2,8]{0,2,1:T(8,128)S(1)} %broadcast_maximum_fusion, pred[512]{0:T(512)(128)(4,1)S(1)} %fusion.28), kind=kLoop, calls=%fused_computation.5 | loop fusion | flops 5240832 | bytes 4211200 | tf_op jit(solution)/shard_map/reduce_sum | solution.py:43
  131.5 0.0 copy-done
  131.5 1.3 divide_convert_fusion
  132.8 1.0 copy.18
  (5 shorter events, 0.0 us)
Async XLA Ops:
  6.5 54.8 %all-gather.4.cloned.1.call-start = ((), (), s32[]{:S(2)}) async-start(), calls=%async_computation | async-start | bytes 2359296 | tf_op jit(solution)/shard_map/all_gather | solution.py:78
  128.0 3.5 %copy-start = (f32[2,512,128,8]{2,1,3,0:T(8,128)S(1)}, f32[2,512,128,8]{2,1,3,0:T(8,128)}, u32[]{:S(2)}) copy-start(f32[2,512,128,8]{2,1,3,0:T(8,128)} %get-tuple-element.8) | copy-start | bytes 12582916
Sparse Core Ops, SparseCore 0:
  9.5 51.7 all-gather.3
where the time goes:
time: 141 us
  blocking collectives  69.1 us (49%)
  waiting for transfers between devices  43.4 us (31%)
  between operations  13.5 us (10%)
  matrix products  6.14 us (4%)
  other arithmetic  4.49 us (3%)
  local copies, waits for them, and re-layouts  4.05 us (3%)
    all_gather x1, waiting for transfers between devices, local(): lax.all_gather(kv_weight, 'blk', axis=1, tiled=True)[0]  43.4 us
    all_gather x1, blocking collectives, local(): lax.all_gather(key_rows, 'blk', axis=0, tiled=True)  30.8 us
    all_gather x1, blocking collectives, local(): lax.all_gather(value_rows, 'blk', axis=0, tiled=True)  30.8 us
    all_gather x1, blocking collectives, local(): lax.all_gather(encoder_states, ('section', 'mp'), axis=0, tiled=True)  7.46 us
    reduce_sum x1, other arithmetic, attend_block(): denominator = jnp.sum(weights, axis=-1)  3.44 us
    unnamed x4, local copies, waits for them, and re-layouts  2.83 us
  transfers between devices with their start and end apart: 1, of which 1 were waited for; matrix products, arithmetic and copies ran while one was open for 2% of the time, Pallas kernels for 0%

commit v1 on v0

v1 whole, which is shorter than its diff:
```python
import functools

import jax
import jax.numpy as jnp
from jax import lax
from jax.experimental import pallas as pl
from jax.experimental.pallas import tpu as pltpu
from jax.sharding import PartitionSpec as P

HEADS = 32
KVH = 4
HD = 128
MEAN = 36
LOG2E = 1.4426950408889634

VMEM_SPEC = pl.BlockSpec(memory_space=pltpu.VMEM)


def normalize(states, norm_gain):
    widened = states.astype(jnp.float32)
    factor = lax.rsqrt(jnp.mean(widened * widened, axis=-1, keepdims=True) + 1e-05)
    return (widened * factor * norm_gain).astype(jnp.bfloat16)


def live_positions(span_len, span_owner, blocks, sections, cores, rows):
    shape = (sections, blocks, cores, rows)
    section, block, core, row = (lax.broadcasted_iota(jnp.int32, shape, axis).reshape(-1) for axis in range(4))
    within = (section * cores + core) * rows + row
    owner = span_owner[:, None]
    length = span_len[:, None]
    load = jnp.sum(jnp.where(owner == block[None, :], length, 0), axis=0)
    before = jnp.sum(jnp.where(owner < block[None, :], length, 0), axis=0)
    return jnp.where(within < load, before + within, -1)[None, :]


def project_kernel(position_ref, rows_ref, weight_ref, partial_ref):
    tiles = weight_ref.shape[1] // HD
    group_rows = partial_ref.shape[1]
    groups = partial_ref.shape[0] // tiles
    position = position_ref[...]
    rows = rows_ref[...]
    weight = weight_ref[...]
    for group in range(groups):
        wanted = lax.broadcasted_iota(jnp.int32, (group_rows, rows.shape[0]), 0) + group * group_rows
        pick = jnp.where(wanted == position, 1.0, 0.0).astype(jnp.bfloat16)
        picked = jnp.dot(pick, rows, preferred_element_type=jnp.float32).astype(jnp.bfloat16)
        projected = jnp.dot(picked, weight, preferred_element_type=jnp.float32).astype(jnp.bfloat16)
        for tile in range(tiles):
            partial_ref[tile * groups + group] = projected[:, tile * HD:(tile + 1) * HD]


def attend_kernel(query_ref, key_ref, value_ref, out_ref):
    heads = query_ref.shape[1] // HD
    keys = key_ref[0]
    values = value_ref[0]
    for head in range(heads):
        span = slice(head * HD, (head + 1) * HD)
        scores = lax.dot_general(
            query_ref[:, span], keys, (((1,), (1,)), ((), ())), preferred_element_type=jnp.float32
        )
        peak = jnp.max(scores, axis=-1, keepdims=True)
        weights = jnp.exp2((scores - peak) * (LOG2E * HD ** -0.5))
        denominator = jnp.sum(weights, axis=-1, keepdims=True)
        numerator = jnp.dot(weights.astype(jnp.bfloat16), values, preferred_element_type=jnp.float32)
        out_ref[:, span] = (numerator / denominator).astype(jnp.bfloat16)


def local(queries, encoder_states, norm_gain, kv_weight, span_len, span_owner):
    sections, blocks, cores = (lax.axis_size(name) for name in ("section", "blk", "mp"))
    rows, width = encoder_states.shape
    depth = width // blocks
    local_groups = kv_weight.shape[3] // HD
    tiles = 2 * local_groups
    groups = blocks // tiles
    group_rows = MEAN * tiles
    query_rows, query_width = queries.shape[1:]
    axes = ("section", "blk", "mp")

    normed = normalize(encoder_states, norm_gain)
    columns = normed.reshape(rows, blocks, depth).transpose(1, 0, 2)
    outgoing = jnp.broadcast_to(columns[None, :, None], (sections, blocks, cores, rows, depth))
    incoming = lax.all_to_all(outgoing.reshape(-1, rows, depth), axes, 0, 0, tiled=True)

    position = live_positions(span_len, span_owner, blocks, sections, cores, rows)
    weight = kv_weight[0].reshape(depth, -1)
    partial = pl.pallas_call(
        project_kernel,
        out_shape=jax.ShapeDtypeStruct((blocks, group_rows, HD), jnp.bfloat16),
        in_specs=[VMEM_SPEC] * 3,
        out_specs=VMEM_SPEC,
        name="project",
    )(position, incoming.reshape(-1, depth), weight)

    exchanged = lax.all_to_all(partial, "blk", 0, 0, tiled=True)
    summed = jnp.sum(exchanged.astype(jnp.float32), axis=0).astype(jnp.bfloat16)
    shared = lax.all_to_all(
        jnp.broadcast_to(summed[None], (blocks, group_rows, HD)), "blk", 0, 0, tiled=True
    )
    keys_values = shared.reshape(tiles, groups * group_rows, HD)
    slots = groups * group_rows
    group_width = query_width // local_groups
    attended = pl.pallas_call(
        attend_kernel,
        grid=(local_groups,),
        out_shape=jax.ShapeDtypeStruct((query_rows, query_width), jnp.bfloat16),
        in_specs=[
            pl.BlockSpec((query_rows, group_width), lambda g: (0, g)),
            pl.BlockSpec((1, slots, HD), lambda g: (g, 0, 0)),
            pl.BlockSpec((1, slots, HD), lambda g: (g + local_groups, 0, 0)),
        ],
        out_specs=pl.BlockSpec((query_rows, group_width), lambda g: (0, g)),
        name="attend",
    )(queries[0], keys_values, keys_values)
    return attended[None]


def solution(mesh):
    in_specs = (
        P("section", "blk", "mp"),
        P(("blk", "section", "mp"), None),
        P(),
        P("section", "blk", None, "mp"),
        P(),
        P(),
    )
    out_specs = P("section", "blk", "mp")
    return jax.shard_map(local, mesh=mesh, in_specs=in_specs, out_specs=out_specs, check_vma=False)
```

time: 141 us -> 57.3 us (0.41)
  blocking collectives: 69.1 us -> 27.6 us
  waiting for transfers between devices: 43.4 us -> 8.59 us
  between operations: 13.5 us -> 0.08 us
  Pallas kernels: 0 us -> 8.33 us
  starting transfers between devices: 0.01 us -> 7.33 us
  matrix products: 6.14 us -> 0 us
  other arithmetic: 4.49 us -> 2.59 us
  local copies, waits for them, and re-layouts: 4.05 us -> 2.42 us
    all_gather x3 -> x0, blocking collectives: 69.1 us -> none  [the longest x1 30.8 us: local(): lax.all_gather(key_rows, 'blk', axis=0, tiled=True)]
    all_gather x1 -> x0, waiting for transfers between devices: 43.4 us -> none  [local(): lax.all_gather(kv_weight, 'blk', axis=1, tiled=True)[0]]
    all_to_all x0 -> x2, blocking collectives: none -> 27.6 us  [the longest x1 14.4 us: local(): exchanged = lax.all_to_all(partial, 'blk', 0, 0, tiled=True)]
    all_to_all x0 -> x1, waiting for transfers between devices: none -> 8.59 us  [local(): lax.all_to_all(outgoing.reshape(-1, rows, depth), axes, 0, 0, tiled=True)]
    pallas_call x0 -> x2, Pallas kernels: none -> 8.33 us  [the longest x1 6.12 us: local(): pl.pallas_call(attend_kernel, grid=(local_groups,), out_shape=jax.ShapeDt...]
    all_to_all x0 -> x1, starting transfers between devices: none -> 7.33 us  [local(): lax.all_to_all(outgoing.reshape(-1, rows, depth), axes, 0, 0, tiled=True)]
    dot_general x3 -> x0, matrix products: 6.14 us -> none  [the longest x1 2.74 us: attend_block(): jnp.einsum('qgjd,rgd->qgjr', query_grid, key_grid, preferred_element_type...]
    reduce_sum x3 -> x2, other arithmetic: 4.32 us -> 0.15 us  [the longest x1 0.1 us: live_positions(): before = jnp.sum(jnp.where(owner < block[None, :], length, 0), axis=0)]
  transfers between devices with their start and end apart: 1 -> 1, of which waited for: 1 -> 1; matrix products, arithmetic and copies ran while one was open for 2% -> 3% of each run, Pallas kernels for 0% -> 0%
where the time goes in v1:
time: 57.3 us; the launch traced here: 56.9 us
  blocking collectives  27.6 us (48%)
  waiting for transfers between devices  8.59 us (15%)
  Pallas kernels  8.33 us (15%)
  starting transfers between devices  7.33 us (13%)
  other arithmetic  2.59 us (5%)
  local copies, waits for them, and re-layouts  2.42 us (4%)
    all_to_all x1, blocking collectives, local(): exchanged = lax.all_to_all(partial, 'blk', 0, 0, tiled=True)  14.4 us
    all_to_all x1, blocking collectives, local(): lax.all_to_all(jnp.broadcast_to(summed[None], (blocks, group_rows, HD)),...  13.1 us
    all_to_all x1, waiting for transfers between devices, local(): lax.all_to_all(outgoing.reshape(-1, rows, depth), axes, 0, 0, tiled=True)  8.59 us
    all_to_all x1, starting transfers between devices, local(): lax.all_to_all(outgoing.reshape(-1, rows, depth), axes, 0, 0, tiled=True)  7.33 us
    pallas_call x1, Pallas kernels, local(): pl.pallas_call(attend_kernel, grid=(local_groups,), out_shape=jax.ShapeDt...  6.12 us
    pallas_call x1, Pallas kernels, local(): pl.pallas_call(project_kernel, out_shape=jax.ShapeDtypeStruct((blocks, gr...  2.2 us
    unnamed x12, local copies, waits for them, and re-layouts  1.45 us
  transfers between devices with their start and end apart: 1, of which 1 were waited for; matrix products, arithmetic and copies ran while one was open for 3% of the time, Pallas kernels for 0%

profile of v1, /device:TPU:0, one launch (start us, length us, event | category | flops | bytes accessed | tf_op | source)
XLA Modules:
  0.0 56.9 jit_solution(1239126239666224985)
XLA Ops:
  0.0 0.0 copy-start.2
  0.0 1.0 %fusion = f32[16]{0:T(128)S(1)} fusion(bf16[16,2048]{1,0:T(8,128)(2,1)} %param.7), kind=kLoop, calls=%fused_computation.2 | loop fusion | flops 98288 | bytes 65600 | tf_op jit(solution)/shard_map/reduce_sum | solution.py:21
  1.1 0.0 copy-done.2
  1.1 0.8 %fusion.2 = bf16[16,2048]{1,0:T(8,128)(2,1)S(1)} fusion(bf16[16,2048]{1,0:T(8,128)(2,1)S(1)} %copy-done.2, f32[2048]{0:T(1024)} %param.8, f32[16]{0:T(128)S(1)} %add_rsqrt_fusion), kind=kLoop, calls=%fused_computation.4 | loop fusion | flops 131072 | bytes 139328 | tf_op jit(solution)/shard_map/convert_element_type | solution.py:22
  1.9 0.7 %broadcast_in_dim.43 = bf16[2,8,2,16,256]{4,3,2,1,0:T(8,128)(2,1)} broadcast(bf16[8,16,256]{2,1,0:T(8,128)(2,1)S(1)} %copy.8), dimensions={1,3,4} | broadcast | bytes 327680 | tf_op jit(solution)/shard_map/broadcast_in_dim | solution.py:81
  2.6 0.0 copy-start.1
  2.6 7.3 %all-to-all-start = ((bf16[32,16,256]{2,1,0:T(8,128)(2,1)}), bf16[32,16,256]{2,1,0:T(8,128)(2,1)S(1)}, u32[]{:S(2)}, u32[]{:S(2)}) async-start(bf16[32,16,256]{2,1,0:T(8,128)(2,1)} %bitcast.4), calls=%async_computation | async-start | bytes 524288 | tf_op jit(solution)/shard_map/all_to_all | solution.py:82
  10.0 0.1 add.50
  10.1 0.1 eq.20
  10.2 0.0 copy-done.1
  10.2 0.0 copy-start.3
  10.2 0.0 copy-start.4
  10.2 0.7 %copy.10 = bf16[32,8,2,256]{3,1,2,0:T(8,128)(2,1)} copy(bf16[32,8,2,256]{3,2,1,0:T(2,128)(2,1)S(1)} %bitcast.19) | data formatting | bytes 524288
  10.9 0.0 copy-done.3
  10.9 0.0 copy-done.4
  10.9 0.1 select_reduce_fusion
  11.0 0.6 %compare_select_fusion.position_ref = s32[1,512]{1,0:T(1,128)} fusion(s32[1,512]{1,0:T(1,128)S(1)} %add.50, s32[1,512]{1,0:T(1,128)S(1)} %bitcast.23, s32[1,512]{1,0:T(1,128)S(1)} %bitcast.22), kind=kLoop, calls=%fused_computation.8 | loop fusion | flops 1536 | bytes 8192 | tf_op jit(solution)/shard_map/jit(_where)/select_n | solution.py:33
  11.6 8.6 %all-to-all-done = bf16[32,16,256]{2,1,0:T(8,128)(2,1)S(1)} async-done(((bf16[32,16,256]{2,1,0:T(8,128)(2,1)}), bf16[32,16,256]{2,1,0:T(8,128)(2,1)S(1)}, u32[]{:S(2)}, u32[]{:S(2)}) %all-to-all-start) | async-done | bytes 262176 | tf_op jit(solution)/shard_map/all_to_all | solution.py:82
  20.2 0.0 copy-start
  20.2 0.7 %copy-done = bf16[32,16,256]{2,1,0:T(8,128)(2,1)} copy-done((bf16[32,16,256]{2,1,0:T(8,128)(2,1)}, bf16[32,16,256]{2,1,0:T(8,128)(2,1)S(1)}, u32[]{:S(2)}) %copy-start) | copy-done | bytes 262168
  20.9 2.2 %project.1 = bf16[8,144,128]{2,1,0:T(8,128)(2,1)} custom-call(s32[1,512]{1,0:T(1,128)} %compare_select_fusion.position_ref, bf16[512,256]{1,0:T(8,128)(2,1)} %bitcast.16, bf16[256,512]{1,0:T(8,128)(2,1)} %bitcast.17), custom_call_target="tpu_custom_call" | custom-call | tf_op jit(solution)/shard_map/project/pallas_call | solution.py:86
  23.1 14.4 %all_to_all.15 = bf16[8,144,128]{2,1,0:T(8,128)(2,1)S(1)} all-to-all(bf16[8,144,128]{2,1,0:T(8,128)(2,1)} %project.1), channel_id=1, replica_groups=mesh['section'=2,'blk'=8,'mp'=2] {'blk'}, dimensions={0} | all-to-all | bytes 589824 | tf_op jit(solution)/shard_map/all_to_all | solution.py:94
  37.6 13.1 %all_to_all.16 = bf16[8,144,128]{2,1,0:T(8,128)(2,1)} all-to-all(bf16[8,144,128]{2,1,0:T(8,128)(2,1)S(1)} %broadcast_in_dim.44), channel_id=1, replica_groups=mesh['section'=2,'blk'=8,'mp'=2] {'blk'}, dimensions={0} | all-to-all | bytes 589824 | tf_op jit(solution)/shard_map/all_to_all | solution.py:96
  50.8 6.1 %attend.1 = bf16[128,2048]{1,0:T(8,128)(2,1)} custom-call(bf16[128,2048]{1,0:T(8,128)(2,1)} %bitcast.18, bf16[4,288,128]{2,1,0:T(8,128)(2,1)} %bitcast.14, bf16[4,288,128]{2,1,0:T(8,128)(2,1)} %bitcast.15), custom_call_target="tpu_custom_call" | custom-call | tf_op jit(solution)/shard_map/attend/pallas_call | solution.py:102
  (7 shorter events, 0.1 us)
Async XLA Ops:
  0.0 1.1 %copy-start.2 = (bf16[16,2048]{1,0:T(8,128)(2,1)S(1)}, bf16[16,2048]{1,0:T(8,128)(2,1)}, u32[]{:S(2)}) copy-start(bf16[16,2048]{1,0:T(8,128)(2,1)} %param.7) | copy-start | bytes 196612
  2.6 7.5 %copy-start.1 = (bf16[1,256,2,256]{3,2,1,0:T(2,128)(2,1)S(1)}, bf16[1,256,2,256]{3,2,1,0:T(2,128)(2,1)}, u32[]{:S(2)}) copy-start(bf16[1,256,2,256]{3,2,1,0:T(2,128)(2,1)} %param.9) | copy-start | bytes 786436
  2.6 17.6 %all-to-all-start = ((bf16[32,16,256]{2,1,0:T(8,128)(2,1)}), bf16[32,16,256]{2,1,0:T(8,128)(2,1)S(1)}, u32[]{:S(2)}, u32[]{:S(2)}) async-start(bf16[32,16,256]{2,1,0:T(8,128)(2,1)} %bitcast.4), calls=%async_computation | async-start | bytes 524288 | tf_op jit(solution)/shard_map/all_to_all | solution.py:82
  10.2 0.8 %copy-start.3 = (s32[64]{0:T(128)S(1)}, s32[64]{0:T(128)}, u32[]{:S(2)}) copy-start(s32[64]{0:T(128)} %param.10) | copy-start | bytes 772
  10.2 0.7 %copy-start.4 = (s32[64]{0:T(128)S(1)}, s32[64]{0:T(128)}, u32[]{:S(2)}) copy-start(s32[64]{0:T(128)} %param.11) | copy-start | bytes 772
  20.2 0.7 %copy-start = (bf16[32,16,256]{2,1,0:T(8,128)(2,1)}, bf16[32,16,256]{2,1,0:T(8,128)(2,1)S(1)}, u32[]{:S(2)}) copy-start(bf16[32,16,256]{2,1,0:T(8,128)(2,1)S(1)} %all-to-all-done) | copy-start | bytes 786436

commit v2 on v1

--- a/solution.py
+++ b/solution.py
@@ -14,12 +14,42 @@
 LOG2E = 1.4426950408889634
 
 VMEM_SPEC = pl.BlockSpec(memory_space=pltpu.VMEM)
+GRANT = pltpu.CompilerParams(vmem_limit_bytes=16 << 20)
 
 
 def normalize(states, norm_gain):
     widened = states.astype(jnp.float32)
     factor = lax.rsqrt(jnp.mean(widened * widened, axis=-1, keepdims=True) + 1e-05)
     return (widened * factor * norm_gain).astype(jnp.bfloat16)
+
+
+def normalize_kernel(states_ref, gain_ref, out_ref):
+    sections, blocks, cores, _, depth = out_ref.shape
+    normed = normalize(states_ref[...], gain_ref[...])
+    for block in range(blocks):
+        columns = normed[:, block * depth:(block + 1) * depth]
+        for section in range(sections):
+            for core in range(cores):
+                out_ref[section, block, core] = columns
+
+
+def column_blocks(states, norm_gain, sections, blocks, cores):
+    rows, width = states.shape
+    depth = width // blocks
+    shape = (sections, blocks, cores, rows, depth)
+    if depth % HD == 0 and rows % 16 == 0:
+        out = pl.pallas_call(
+            normalize_kernel,
+            out_shape=jax.ShapeDtypeStruct(shape, jnp.bfloat16),
+            in_specs=[VMEM_SPEC] * 2,
+            out_specs=VMEM_SPEC,
+            compiler_params=GRANT,
+            name="normalize",
+        )(states, norm_gain[None, :])
+    else:
+        columns = normalize(states, norm_gain).reshape(rows, blocks, depth).transpose(1, 0, 2)
+        out = jnp.broadcast_to(columns[None, :, None], shape)
+    return out.reshape(-1, rows, depth)
 
 
 def live_positions(span_len, span_owner, blocks, sections, cores, rows):
@@ -40,29 +70,42 @@
     position = position_ref[...]
     rows = rows_ref[...]
     weight = weight_ref[...]
-    for group in range(groups):
-        wanted = lax.broadcasted_iota(jnp.int32, (group_rows, rows.shape[0]), 0) + group * group_rows
+    step = 2 if groups % 2 == 0 else 1
+    for first in range(0, groups, step):
+        wanted = lax.broadcasted_iota(jnp.int32, (step * group_rows, rows.shape[0]), 0) + first * group_rows
         pick = jnp.where(wanted == position, 1.0, 0.0).astype(jnp.bfloat16)
         picked = jnp.dot(pick, rows, preferred_element_type=jnp.float32).astype(jnp.bfloat16)
         projected = jnp.dot(picked, weight, preferred_element_type=jnp.float32).astype(jnp.bfloat16)
-        for tile in range(tiles):
-            partial_ref[tile * groups + group] = projected[:, tile * HD:(tile + 1) * HD]
+        for group in range(step):
+            for tile in range(tiles):
+                partial_ref[tile * groups + first + group] = projected[
+                    group * group_rows:(group + 1) * group_rows, tile * HD:(tile + 1) * HD
+                ]
+
+
+def sum_kernel(parts_ref, out_ref):
+    total = parts_ref[0].astype(jnp.float32)
+    for part in range(1, parts_ref.shape[0]):
+        total += parts_ref[part].astype(jnp.float32)
+    total = total.astype(jnp.bfloat16)
+    for part in range(out_ref.shape[0]):
+        out_ref[part] = total
 
 
 def attend_kernel(query_ref, key_ref, value_ref, out_ref):
     heads = query_ref.shape[1] // HD
-    keys = key_ref[0]
-    values = value_ref[0]
+    count = query_ref.shape[0]
+    stacked = jnp.concatenate([query_ref[:, head * HD:(head + 1) * HD] for head in range(heads)], axis=0)
+    scores = lax.dot_general(
+        stacked, key_ref[0], (((1,), (1,)), ((), ())), preferred_element_type=jnp.float32
+    )
+    peak = jnp.max(scores, axis=-1, keepdims=True)
+    weights = jnp.exp2((scores - peak) * (LOG2E * HD ** -0.5))
+    denominator = jnp.sum(weights, axis=-1, keepdims=True)
+    numerator = jnp.dot(weights.astype(jnp.bfloat16), value_ref[0], preferred_element_type=jnp.float32)
+    attended = (numerator * (1.0 / denominator)).astype(jnp.bfloat16)
     for head in range(heads):
-        span = slice(head * HD, (head + 1) * HD)
-        scores = lax.dot_general(
-            query_ref[:, span], keys, (((1,), (1,)), ((), ())), preferred_element_type=jnp.float32
-        )
-        peak = jnp.max(scores, axis=-1, keepdims=True)
-        weights = jnp.exp2((scores - peak) * (LOG2E * HD ** -0.5))
-        denominator = jnp.sum(weights, axis=-1, keepdims=True)
-        numerator = jnp.dot(weights.astype(jnp.bfloat16), values, preferred_element_type=jnp.float32)
-        out_ref[:, span] = (numerator / denominator).astype(jnp.bfloat16)
+        out_ref[:, head * HD:(head + 1) * HD] = attended[head * count:(head + 1) * count]
 
 
 def local(queries, encoder_states, norm_gain, kv_weight, span_len, span_owner):
@@ -76,10 +119,8 @@
     query_rows, query_width = queries.shape[1:]
     axes = ("section", "blk", "mp")
 
-    normed = normalize(encoder_states, norm_gain)
-    columns = normed.reshape(rows, blocks, depth).transpose(1, 0, 2)
-    outgoing = jnp.broadcast_to(columns[None, :, None], (sections, blocks, cores, rows, depth))
-    incoming = lax.all_to_all(outgoing.reshape(-1, rows, depth), axes, 0, 0, tiled=True)
+    outgoing = column_blocks(encoder_states, norm_gain, sections, blocks, cores)
+    incoming = lax.all_to_all(outgoing, axes, 0, 0, tiled=True)
 
     position = live_positions(span_len, span_owner, blocks, sections, cores, rows)
     weight = kv_weight[0].reshape(depth, -1)
@@ -88,14 +129,20 @@
         out_shape=jax.ShapeDtypeStruct((blocks, group_rows, HD), jnp.bfloat16),
         in_specs=[VMEM_SPEC] * 3,
         out_specs=VMEM_SPEC,
+        compiler_params=GRANT,
         name="project",
     )(position, incoming.reshape(-1, depth), weight)
 
     exchanged = lax.all_to_all(partial, "blk", 0, 0, tiled=True)
-    summed = jnp.sum(exchanged.astype(jnp.float32), axis=0).astype(jnp.bfloat16)
-    shared = lax.all_to_all(
-        jnp.broadcast_to(summed[None], (blocks, group_rows, HD)), "blk", 0, 0, tiled=True
-    )
+    summed = pl.pallas_call(
+        sum_kernel,
+        out_shape=jax.ShapeDtypeStruct((blocks, group_rows, HD), jnp.bfloat16),
+        in_specs=[VMEM_SPEC],
+        out_specs=VMEM_SPEC,
+        compiler_params=GRANT,
+        name="sum",
+    )(exchanged)
+    shared = lax.all_to_all(summed, "blk", 0, 0, tiled=True)
     keys_values = shared.reshape(tiles, groups * group_rows, HD)
     slots = groups * group_rows
     group_width = query_width // local_groups
@@ -109,6 +156,7 @@
             pl.BlockSpec((1, slots, HD), lambda g: (g + local_groups, 0, 0)),
         ],
         out_specs=pl.BlockSpec((query_rows, group_width), lambda g: (0, g)),
+        compiler_params=GRANT,
         name="attend",
     )(queries[0], keys_values, keys_values)
     return attended[None]

time: 57.3 us -> 49.4 us (0.86)
  Pallas kernels: 8.33 us -> 3.45 us
  other arithmetic: 2.59 us -> 0.12 us
  blocking collectives: 27.6 us -> 26.4 us
  waiting for transfers between devices: 8.59 us -> 9.26 us
    pallas_call x1, Pallas kernels: 6.12 us -> 2.09 us  [local(): pl.pallas_call(attend_kernel, grid=(local_groups,), out_shape=jax.ShapeDt...]
    pallas_call x1, Pallas kernels: 2.2 us -> 0.49 us  [local(): pl.pallas_call(project_kernel, out_shape=jax.ShapeDtypeStruct((blocks, gr...]
    reduce_sum x2 -> x0, other arithmetic: 1.08 us -> none  [the longest x1 1.04 us: normalize(): jnp.mean(widened * widened, axis=-1, keepdims=True) + 1e-05]
    all_to_all x1, blocking collectives: 14.4 us -> 13.5 us  [local(): exchanged = lax.all_to_all(partial, 'blk', 0, 0, tiled=True)]
    pallas_call x0 -> x2, Pallas kernels: none -> 0.87 us  [the longest x1 0.82 us: column_blocks(): pl.pallas_call(normalize_kernel, out_shape=jax.ShapeDtypeStruct(shape, jn...]
    convert_element_type x1 -> x0, other arithmetic: 0.78 us -> none  [normalize(): return (widened * factor * norm_gain).astype(jnp.bfloat16)]
    broadcast_in_dim x2 -> x0, local copies, waits for them, and re-layouts: 0.76 us -> none  [the longest x1 0.72 us: local(): jnp.broadcast_to(columns[None, :, None], (sections, blocks, cores, rows,...]
    unnamed x12 -> x13, local copies, waits for them, and re-layouts: 1.45 us -> 2.2 us
  transfers between devices with their start and end apart: 1 -> 1, of which waited for: 1 -> 1; matrix products, arithmetic and copies ran while one was open for 3% -> 1% of each run, Pallas kernels for 0% -> 0%
where the time goes in v2:
time: 49.4 us; the launch traced here: 49 us
  blocking collectives  26.4 us (53%)
  waiting for transfers between devices  9.26 us (19%)
  starting transfers between devices  7.33 us (15%)
  Pallas kernels  3.45 us (7%)
  local copies, waits for them, and re-layouts  2.39 us (5%)
    all_to_all x1, blocking collectives, local(): exchanged = lax.all_to_all(partial, 'blk', 0, 0, tiled=True)  13.5 us
    all_to_all x1, blocking collectives, local(): shared = lax.all_to_all(summed, 'blk', 0, 0, tiled=True)  13 us
    all_to_all x1, waiting for transfers between devices, local(): incoming = lax.all_to_all(outgoing, axes, 0, 0, tiled=True)  9.26 us
    all_to_all x1, starting transfers between devices, local(): incoming = lax.all_to_all(outgoing, axes, 0, 0, tiled=True)  7.33 us
    unnamed x13, local copies, waits for them, and re-layouts  2.2 us
    pallas_call x1, Pallas kernels, local(): pl.pallas_call(attend_kernel, grid=(local_groups,), out_shape=jax.ShapeDt...  2.09 us
  transfers between devices with their start and end apart: 1, of which 1 were waited for; matrix products, arithmetic and copies ran while one was open for 1% of the time, Pallas kernels for 0%

profile of v2, /device:TPU:0, one launch (start us, length us, event | category | flops | bytes accessed | tf_op | source)
XLA Modules:
  0.0 49.0 jit_solution(1066231027163428237)
XLA Ops:
  0.0 0.0 copy-start.1
  0.0 0.8 %copy-done.1 = bf16[16,2048]{1,0:T(8,128)(2,1)S(1)} copy-done((bf16[16,2048]{1,0:T(8,128)(2,1)S(1)}, bf16[16,2048]{1,0:T(8,128)(2,1)}, u32[]{:S(2)}) %copy-start.1) | copy-done | bytes 65560
  0.8 0.0 copy-start.2
  0.8 0.7 %copy-done.2 = f32[2048]{0:T(1024)S(1)} copy-done((f32[2048]{0:T(1024)S(1)}, f32[2048]{0:T(1024)}, u32[]{:S(2)}) %copy-start.2) | copy-done | bytes 8216
  1.5 0.8 %normalize.1 = bf16[2,8,2,16,256]{4,3,2,1,0:T(8,128)(2,1)} custom-call(bf16[16,2048]{1,0:T(8,128)(2,1)S(1)} %copy-done.1, f32[1,2048]{1,0:T(1,128)S(1)} %bitcast.16), custom_call_target="tpu_custom_call" | custom-call | tf_op jit(solution)/shard_map/normalize/pallas_call | solution.py:41
  2.4 0.0 copy-start.3
  2.4 7.3 %all-to-all-start = ((bf16[32,16,256]{2,1,0:T(8,128)(2,1)}), bf16[32,16,256]{2,1,0:T(8,128)(2,1)S(1)}, u32[]{:S(2)}, u32[]{:S(2)}) async-start(bf16[32,16,256]{2,1,0:T(8,128)(2,1)} %bitcast.4), calls=%async_computation | async-start | bytes 524288 | tf_op jit(solution)/shard_map/all_to_all | solution.py:123
  9.7 0.1 add.42
  9.8 0.1 eq.20
  9.9 0.0 copy-done.3
  9.9 0.0 copy-start.4
  9.9 0.0 copy-start.5
  10.0 0.6 %copy-done.4 = s32[64]{0:T(128)S(1)} copy-done((s32[64]{0:T(128)S(1)}, s32[64]{0:T(128)}, u32[]{:S(2)}) %copy-start.4) | copy-done | bytes 280
  10.6 0.0 copy-done.5
  10.6 0.1 select_reduce_fusion
  10.7 9.3 %all-to-all-done = bf16[32,16,256]{2,1,0:T(8,128)(2,1)S(1)} async-done(((bf16[32,16,256]{2,1,0:T(8,128)(2,1)}), bf16[32,16,256]{2,1,0:T(8,128)(2,1)S(1)}, u32[]{:S(2)}, u32[]{:S(2)}) %all-to-all-start) | async-done | bytes 262176 | tf_op jit(solution)/shard_map/all_to_all | solution.py:123
  20.0 0.5 %project.1 = bf16[8,144,128]{2,1,0:T(8,128)(2,1)S(1)} custom-call(s32[1,512]{1,0:T(1,128)S(1)} %compare_select_fusion.position_ref, bf16[512,256]{1,0:T(8,128)(2,1)S(1)} %bitcast.13, bf16[256,512]{1,0:T(8,128)(2,1)S(1)} %bitcast.14), custom_call_target="tpu_custom_call" | custom-call | tf_op jit(solution)/shard_map/project/pallas_call | solution.py:127
  20.5 13.5 %all_to_all.15.parts_ref = bf16[8,144,128]{2,1,0:T(8,128)(2,1)S(1)} all-to-all(bf16[8,144,128]{2,1,0:T(8,128)(2,1)S(1)} %project.1), channel_id=1, replica_groups=mesh['section'=2,'blk'=8,'mp'=2] {'blk'}, dimensions={0} | all-to-all | bytes 589824 | tf_op jit(solution)/shard_map/all_to_all | solution.py:136
  33.9 0.0 copy-start
  34.0 13.0 %all_to_all.16 = bf16[8,144,128]{2,1,0:T(8,128)(2,1)S(1)} all-to-all(bf16[8,144,128]{2,1,0:T(8,128)(2,1)S(1)} %sum.1), channel_id=1, replica_groups=mesh['section'=2,'blk'=8,'mp'=2] {'blk'}, dimensions={0} | all-to-all | bytes 589824 | tf_op jit(solution)/shard_map/all_to_all | solution.py:145
  47.0 0.0 copy-done
  47.0 2.1 %attend.1 = bf16[128,2048]{1,0:T(8,128)(2,1)} custom-call(bf16[128,2048]{1,0:T(8,128)(2,1)S(1)} %bitcast.15, bf16[4,288,128]{2,1,0:T(8,128)(2,1)S(1)} %bitcast.11, bf16[4,288,128]{2,1,0:T(8,128)(2,1)S(1)} %bitcast.12), custom_call_target="tpu_custom_call" | custom-call | tf_op jit(solution)/shard_map/attend/pallas_call | solution.py:149
  (5 shorter events, 0.1 us)
Async XLA Ops:
  0.0 0.8 %copy-start.1 = (bf16[16,2048]{1,0:T(8,128)(2,1)S(1)}, bf16[16,2048]{1,0:T(8,128)(2,1)}, u32[]{:S(2)}) copy-start(bf16[16,2048]{1,0:T(8,128)(2,1)} %states_ref.1) | copy-start | bytes 196612
  0.8 0.7 %copy-start.2 = (f32[2048]{0:T(1024)S(1)}, f32[2048]{0:T(1024)}, u32[]{:S(2)}) copy-start(f32[2048]{0:T(1024)} %param.8) | copy-start | bytes 24580
  2.4 7.5 %copy-start.3 = (bf16[1,256,2,256]{3,2,1,0:T(2,128)(2,1)S(1)}, bf16[1,256,2,256]{3,2,1,0:T(2,128)(2,1)}, u32[]{:S(2)}) copy-start(bf16[1,256,2,256]{3,2,1,0:T(2,128)(2,1)} %param.9) | copy-start | bytes 786436
  2.4 17.6 %all-to-all-start = ((bf16[32,16,256]{2,1,0:T(8,128)(2,1)}), bf16[32,16,256]{2,1,0:T(8,128)(2,1)S(1)}, u32[]{:S(2)}, u32[]{:S(2)}) async-start(bf16[32,16,256]{2,1,0:T(8,128)(2,1)} %bitcast.4), calls=%async_computation | async-start | bytes 524288 | tf_op jit(solution)/shard_map/all_to_all | solution.py:123
  9.9 0.7 %copy-start.4 = (s32[64]{0:T(128)S(1)}, s32[64]{0:T(128)}, u32[]{:S(2)}) copy-start(s32[64]{0:T(128)} %param.10) | copy-start | bytes 772
  9.9 0.7 %copy-start.5 = (s32[64]{0:T(128)S(1)}, s32[64]{0:T(128)}, u32[]{:S(2)}) copy-start(s32[64]{0:T(128)} %param.11) | copy-start | bytes 772
  33.9 13.0 %copy-start = (bf16[1,128,2048]{2,1,0:T(8,128)(2,1)S(1)}, bf16[1,128,2048]{2,1,0:T(8,128)(2,1)}, u32[]{:S(2)}) copy-start(bf16[1,128,2048]{2,1,0:T(8,128)(2,1)} %param.6) | copy-start | bytes 1572868

commit v3 on v2

--- a/solution.py
+++ b/solution.py
@@ -1,5 +1,3 @@
-import functools
-
 import jax
 import jax.numpy as jnp
 from jax import lax
@@ -7,8 +5,6 @@
 from jax.experimental.pallas import tpu as pltpu
 from jax.sharding import PartitionSpec as P
 
-HEADS = 32
-KVH = 4
 HD = 128
 MEAN = 36
 LOG2E = 1.4426950408889634
@@ -24,37 +20,41 @@
 
 
 def normalize_kernel(states_ref, gain_ref, out_ref):
-    sections, blocks, cores, _, depth = out_ref.shape
+    sections, blocks, _, width = out_ref.shape
+    depth = width // 2
     normed = normalize(states_ref[...], gain_ref[...])
     for block in range(blocks):
-        columns = normed[:, block * depth:(block + 1) * depth]
+        partner = (block + blocks // 2) % blocks
         for section in range(sections):
-            for core in range(cores):
-                out_ref[section, block, core] = columns
+            out_ref[section, block, :, :depth] = normed[:, block * depth:(block + 1) * depth]
+            out_ref[section, block, :, depth:] = normed[:, partner * depth:(partner + 1) * depth]
 
 
-def column_blocks(states, norm_gain, sections, blocks, cores):
+def column_blocks(states, norm_gain, sections, blocks):
     rows, width = states.shape
     depth = width // blocks
-    shape = (sections, blocks, cores, rows, depth)
+    shape = (sections, blocks, rows, 2 * depth)
     if depth % HD == 0 and rows % 16 == 0:
         out = pl.pallas_call(
             normalize_kernel,
             out_shape=jax.ShapeDtypeStruct(shape, jnp.bfloat16),
             in_specs=[VMEM_SPEC] * 2,
             out_specs=VMEM_SPEC,
-            compiler_params=GRANT,
+            compiler_params=pltpu.CompilerParams(vmem_limit_bytes=60 << 20),
             name="normalize",
         )(states, norm_gain[None, :])
     else:
         columns = normalize(states, norm_gain).reshape(rows, blocks, depth).transpose(1, 0, 2)
-        out = jnp.broadcast_to(columns[None, :, None], shape)
-    return out.reshape(-1, rows, depth)
+        columns = jnp.concatenate([columns, jnp.roll(columns, -(blocks // 2), axis=0)], axis=2)
+        out = jnp.broadcast_to(columns[None], shape)
+    return out.reshape(-1, rows, 2 * depth)
 
 
-def live_positions(span_len, span_owner, blocks, sections, cores, rows):
-    shape = (sections, blocks, cores, rows)
-    section, block, core, row = (lax.broadcasted_iota(jnp.int32, shape, axis).reshape(-1) for axis in range(4))
+def live_positions(span_len, span_owner, blocks, sections, cores, rows, core):
+    index = lax.iota(jnp.int32, sections * blocks * rows)
+    row = index % rows
+    block = index // rows % blocks
+    section = index // (rows * blocks)
     within = (section * cores + core) * rows + row
     owner = span_owner[:, None]
     length = span_len[:, None]
@@ -63,24 +63,27 @@
     return jnp.where(within < load, before + within, -1)[None, :]
 
 
-def project_kernel(position_ref, rows_ref, weight_ref, partial_ref):
-    tiles = weight_ref.shape[1] // HD
+def project_kernel(
+    own_position_ref, other_position_ref, own_rows_ref, other_rows_ref, own_weight_ref, other_weight_ref, partial_ref
+):
+    depth, width = own_weight_ref.shape
+    tiles = width // HD
     group_rows = partial_ref.shape[1]
     groups = partial_ref.shape[0] // tiles
-    position = position_ref[...]
-    rows = rows_ref[...]
-    weight = weight_ref[...]
-    step = 2 if groups % 2 == 0 else 1
-    for first in range(0, groups, step):
-        wanted = lax.broadcasted_iota(jnp.int32, (step * group_rows, rows.shape[0]), 0) + first * group_rows
-        pick = jnp.where(wanted == position, 1.0, 0.0).astype(jnp.bfloat16)
-        picked = jnp.dot(pick, rows, preferred_element_type=jnp.float32).astype(jnp.bfloat16)
-        projected = jnp.dot(picked, weight, preferred_element_type=jnp.float32).astype(jnp.bfloat16)
-        for group in range(step):
-            for tile in range(tiles):
-                partial_ref[tile * groups + first + group] = projected[
-                    group * group_rows:(group + 1) * group_rows, tile * HD:(tile + 1) * HD
-                ]
+    own_rows, other_rows = own_rows_ref[...], other_rows_ref[...]
+    own_weight, other_weight = own_weight_ref[...], other_weight_ref[...]
+    for group in range(groups):
+        wanted = lax.broadcasted_iota(jnp.int32, (group_rows, own_rows.shape[0]), 0) + group * group_rows
+        own_pick = jnp.where(wanted == own_position_ref[...], 1.0, 0.0).astype(jnp.bfloat16)
+        other_pick = jnp.where(wanted == other_position_ref[...], 1.0, 0.0).astype(jnp.bfloat16)
+        picked = jnp.dot(own_pick, own_rows, preferred_element_type=jnp.float32)
+        picked += jnp.dot(other_pick, other_rows, preferred_element_type=jnp.float32)
+        picked = picked.astype(jnp.bfloat16)
+        projected = jnp.dot(picked[:, :depth], own_weight, preferred_element_type=jnp.float32)
+        projected += jnp.dot(picked[:, depth:], other_weight, preferred_element_type=jnp.float32)
+        projected = projected.astype(jnp.bfloat16)
+        for tile in range(tiles):
+            partial_ref[tile * groups + group] = projected[:, tile * HD:(tile + 1) * HD]
 
 
 def sum_kernel(parts_ref, out_ref):
@@ -114,35 +117,47 @@
     depth = width // blocks
     local_groups = kv_weight.shape[3] // HD
     tiles = 2 * local_groups
-    groups = blocks // tiles
-    group_rows = MEAN * tiles
+    half = blocks // 2
+    groups = half // tiles
+    group_rows = MEAN * blocks // groups
     query_rows, query_width = queries.shape[1:]
-    axes = ("section", "blk", "mp")
+    halves = [list(range(half)), list(range(half, blocks))]
+    core = lax.axis_index("mp")
 
-    outgoing = column_blocks(encoder_states, norm_gain, sections, blocks, cores)
-    incoming = lax.all_to_all(outgoing, axes, 0, 0, tiled=True)
+    other_weight = lax.ppermute(kv_weight, "blk", [(b, (b + half) % blocks) for b in range(blocks)])
+    outgoing = column_blocks(encoder_states, norm_gain, sections, blocks)
+    own_rows = lax.all_to_all(outgoing, ("section", "blk"), 0, 0, tiled=True)
+    other_rows = lax.ppermute(own_rows, "mp", [(c, (c + 1) % cores) for c in range(cores)])
 
-    position = live_positions(span_len, span_owner, blocks, sections, cores, rows)
-    weight = kv_weight[0].reshape(depth, -1)
+    own_position = live_positions(span_len, span_owner, blocks, sections, cores, rows, core)
+    other_position = live_positions(span_len, span_owner, blocks, sections, cores, rows, cores - 1 - core)
+    part_shape = jax.ShapeDtypeStruct((half, group_rows, HD), jnp.bfloat16)
     partial = pl.pallas_call(
         project_kernel,
-        out_shape=jax.ShapeDtypeStruct((blocks, group_rows, HD), jnp.bfloat16),
-        in_specs=[VMEM_SPEC] * 3,
+        out_shape=part_shape,
+        in_specs=[VMEM_SPEC] * 6,
         out_specs=VMEM_SPEC,
         compiler_params=GRANT,
         name="project",
-    )(position, incoming.reshape(-1, depth), weight)
+    )(
+        own_position,
+        other_position,
+        own_rows.reshape(-1, 2 * depth),
+        other_rows.reshape(-1, 2 * depth),
+        kv_weight[0].reshape(depth, -1),
+        other_weight[0].reshape(depth, -1),
+    )
 
-    exchanged = lax.all_to_all(partial, "blk", 0, 0, tiled=True)
+    exchanged = lax.all_to_all(partial, "blk", 0, 0, tiled=True, axis_index_groups=halves)
     summed = pl.pallas_call(
         sum_kernel,
-        out_shape=jax.ShapeDtypeStruct((blocks, group_rows, HD), jnp.bfloat16),
+        out_shape=part_shape,
         in_specs=[VMEM_SPEC],
         out_specs=VMEM_SPEC,
         compiler_params=GRANT,
         name="sum",
     )(exchanged)
-    shared = lax.all_to_all(summed, "blk", 0, 0, tiled=True)
+    shared = lax.all_to_all(summed, "blk", 0, 0, tiled=True, axis_index_groups=halves)
     keys_values = shared.reshape(tiles, groups * group_rows, HD)
     slots = groups * group_rows
     group_width = query_width // local_groups

time: 49.4 us -> 50.6 us (1.024)
  blocking collectives: 26.4 us -> 17.4 us
  waiting for transfers between devices: 9.26 us -> 16.9 us
  starting transfers between devices: 7.33 us -> 11.4 us
  local copies, waits for them, and re-layouts: 2.39 us -> 0.08 us
  Pallas kernels: 3.45 us -> 4.34 us
    all_to_all x2, blocking collectives: 26.4 us -> 17.4 us  [the longest x1 8.7 us: local(): lax.all_to_all(partial, 'blk', 0, 0, tiled=True, axis_index_groups=halves)]
    all_to_all x1, waiting for transfers between devices: 9.26 us -> 13.3 us  [local(): own_rows = lax.all_to_all(outgoing, ('section', 'blk'), 0, 0, tiled=True)]
    ppermute x0 -> x2, waiting for transfers between devices: none -> 3.62 us  [the longest x1 3.62 us: local(): lax.ppermute(kv_weight, 'blk', [(b, (b + half) % blocks) for b in range(b...]
    ppermute x0 -> x2, starting transfers between devices: none -> 2.89 us  [the longest x1 2.89 us: local(): lax.ppermute(kv_weight, 'blk', [(b, (b + half) % blocks) for b in range(b...]
    unnamed x13 -> x10, local copies, waits for them, and re-layouts: 2.2 us -> 0.08 us
    all_to_all x1, starting transfers between devices: 7.33 us -> 8.47 us  [local(): own_rows = lax.all_to_all(outgoing, ('section', 'blk'), 0, 0, tiled=True)]
    pallas_call x1, Pallas kernels: 0.82 us -> 1.67 us  [column_blocks(): pl.pallas_call(normalize_kernel, out_shape=jax.ShapeDtypeStruct(shape, jn...]
  transfers between devices with their start and end apart: 1 -> 3, of which waited for: 1 -> 2; matrix products, arithmetic and copies ran while one was open for 1% -> 0% of each run, Pallas kernels for 0% -> 0%
where the time goes in v3:
time: 50.6 us; the launch traced here: 50.2 us
  blocking collectives  17.4 us (34%)
  waiting for transfers between devices  16.9 us (33%)
  starting transfers between devices  11.4 us (23%)
  Pallas kernels  4.34 us (9%)
    all_to_all x1, waiting for transfers between devices, local(): own_rows = lax.all_to_all(outgoing, ('section', 'blk'), 0, 0, tiled=True)  13.3 us
    all_to_all x1, blocking collectives, local(): lax.all_to_all(partial, 'blk', 0, 0, tiled=True, axis_index_groups=halves)  8.7 us
    all_to_all x1, blocking collectives, local(): lax.all_to_all(summed, 'blk', 0, 0, tiled=True, axis_index_groups=halves)  8.66 us
    all_to_all x1, starting transfers between devices, local(): own_rows = lax.all_to_all(outgoing, ('section', 'blk'), 0, 0, tiled=True)  8.47 us
    ppermute x1, waiting for transfers between devices, local(): lax.ppermute(kv_weight, 'blk', [(b, (b + half) % blocks) for b in range(b...  3.62 us
    ppermute x1, starting transfers between devices, local(): lax.ppermute(kv_weight, 'blk', [(b, (b + half) % blocks) for b in range(b...  2.89 us
    pallas_call x1, Pallas kernels, local(): pl.pallas_call(attend_kernel, grid=(local_groups,), out_shape=jax.ShapeDt...  2.09 us
    pallas_call x1, Pallas kernels, column_blocks(): pl.pallas_call(normalize_kernel, out_shape=jax.ShapeDtypeStruct(shape, jn...  1.67 us
  transfers between devices with their start and end apart: 3, of which 2 were waited for; matrix products, arithmetic and copies ran while one was open for 0% of the time, Pallas kernels for 0%

profile of v3, /device:TPU:0, one launch (start us, length us, event | category | flops | bytes accessed | tf_op | source)
XLA Modules:
  0.0 50.2 jit_solution(2622692430140808762)
XLA Ops:
  0.0 1.7 %normalize.1 = bf16[2,8,16,512]{3,2,1,0:T(8,128)(2,1)} custom-call(bf16[16,2048]{1,0:T(8,128)(2,1)} %states_ref.1, f32[1,2048]{1,0:T(1,128)} %bitcast.22), custom_call_target="tpu_custom_call" | custom-call | tf_op jit(solution)/shard_map/normalize/pallas_call | solution.py:38
  1.7 0.0 copy-start.1
  1.7 8.5 %all-to-all-start = ((bf16[16,16,512]{2,1,0:T(8,128)(2,1)}), bf16[16,16,512]{2,1,0:T(8,128)(2,1)S(1)}, u32[]{:S(2)}, u32[]{:S(2)}) async-start(bf16[16,16,512]{2,1,0:T(8,128)(2,1)} %bitcast.19), calls=%async_computation | async-start | bytes 524288 | tf_op jit(solution)/shard_map/all_to_all | solution.py:129
  10.2 0.0 copy-done.1
  10.2 0.0 copy-start.2
  10.2 0.0 copy-start.3
  10.2 2.9 %collective-permute-start.1 = (bf16[1,256,2,256]{3,2,1,0:T(2,128)(2,1)S(1)}, bf16[1,256,2,256]{3,2,1,0:T(2,128)(2,1)S(1)}, u32[]{:S(2)}, u32[]{:S(2)}) collective-permute-start(bf16[1,256,2,256]{3,2,1,0:T(2,128)(2,1)S(1)} %copy-done.1), channel_id=1, source_target_pairs={{0,8},{2,10},{4,12},{6,14},{8,0},{10,2},{12,4},{14,6},{1,9},{3,11}... | collective-permute-start | bytes 786440 | tf_op jit(solution)/shard_map/ppermute | solution.py:127
  13.1 13.3 %all-to-all-done = bf16[16,16,512]{2,1,0:T(8,128)(2,1)S(1)} async-done(((bf16[16,16,512]{2,1,0:T(8,128)(2,1)}), bf16[16,16,512]{2,1,0:T(8,128)(2,1)S(1)}, u32[]{:S(2)}, u32[]{:S(2)}) %all-to-all-start) | async-done | bytes 262176 | tf_op jit(solution)/shard_map/all_to_all | solution.py:129
  26.4 0.0 collective-permute-start
  26.4 0.0 copy-done.2
  26.4 0.0 copy-done.3
  26.4 0.1 select_reduce_fusion
  26.5 3.6 %collective-permute-done.1 = bf16[1,256,2,256]{3,2,1,0:T(2,128)(2,1)S(1)} collective-permute-done((bf16[1,256,2,256]{3,2,1,0:T(2,128)(2,1)S(1)}, bf16[1,256,2,256]{3,2,1,0:T(2,128)(2,1)S(1)}, u32[]{:S(2)}, u32[]{:S(2)}) %collective-permute-start.1) | collective-permute-done | bytes 262176 | tf_op jit(solution)/shard_map/ppermute | solution.py:127
  30.2 0.0 collective-permute-done
  30.2 0.5 %project.1 = bf16[4,288,128]{2,1,0:T(8,128)(2,1)S(1)} custom-call(s32[1,256]{1,0:T(1,128)S(1)} %get-tuple-element.8.own_position_ref, s32[1,256]{1,0:T(1,128)S(1)} %get-tuple-element.7.other_position_ref, bf16[256,512]{1,0:T(8,128)(2,1)S(1)} %bitcast.14, bf16[256,512]{1,0:T(8,128)(2,1)S(1)} %bitcast.18, bf16[256,512]{1,0:T(8,128)(2,1)S(1)} %bitcast.15, ...), custom_call_target="tpu_custom_call" | custom-call | tf_op jit(solution)/shard_map/project/pallas_call | solution.py:135
  30.8 8.7 %all_to_all.15.parts_ref = bf16[4,288,128]{2,1,0:T(8,128)(2,1)S(1)} all-to-all(bf16[4,288,128]{2,1,0:T(8,128)(2,1)S(1)} %project.1), channel_id=1, replica_groups={{0,2,4,6},{8,10,12,14},{1,3,5,7},{9,11,13,15},{16,18,20,22},{24,26,28,3..., dimensions={0} | all-to-all | bytes 589824 | tf_op jit(solution)/shard_map/all_to_all | solution.py:151
  39.4 0.0 copy-start
  39.5 8.7 %all_to_all.16.key_ref.value_ref = bf16[4,288,128]{2,1,0:T(8,128)(2,1)S(1)} all-to-all(bf16[4,288,128]{2,1,0:T(8,128)(2,1)S(1)} %sum.1), channel_id=1, replica_groups={{0,2,4,6},{8,10,12,14},{1,3,5,7},{9,11,13,15},{16,18,20,22},{24,26,28,3..., dimensions={0} | all-to-all | bytes 589824 | tf_op jit(solution)/shard_map/all_to_all | solution.py:160
  48.2 0.0 copy-done
  48.2 2.1 %attend.1 = bf16[128,2048]{1,0:T(8,128)(2,1)} custom-call(bf16[128,2048]{1,0:T(8,128)(2,1)S(1)} %bitcast.17, bf16[4,288,128]{2,1,0:T(8,128)(2,1)S(1)} %all_to_all.16.key_ref.value_ref, bf16[4,288,128]{2,1,0:T(8,128)(2,1)S(1)} %all_to_all.16.key_ref.value_ref), custom_call_target="tpu_custom_call" | custom-call | tf_op jit(solution)/shard_map/attend/pallas_call | solution.py:164
  (5 shorter events, 0.1 us)
Async XLA Ops:
  1.7 8.5 %copy-start.1 = (bf16[1,256,2,256]{3,2,1,0:T(2,128)(2,1)S(1)}, bf16[1,256,2,256]{3,2,1,0:T(2,128)(2,1)}, u32[]{:S(2)}) copy-start(bf16[1,256,2,256]{3,2,1,0:T(2,128)(2,1)} %param.9) | copy-start | bytes 786436
  1.7 24.7 %all-to-all-start = ((bf16[16,16,512]{2,1,0:T(8,128)(2,1)}), bf16[16,16,512]{2,1,0:T(8,128)(2,1)S(1)}, u32[]{:S(2)}, u32[]{:S(2)}) async-start(bf16[16,16,512]{2,1,0:T(8,128)(2,1)} %bitcast.19), calls=%async_computation | async-start | bytes 524288 | tf_op jit(solution)/shard_map/all_to_all | solution.py:129
  10.2 16.2 %copy-start.2 = (s32[64]{0:T(128)S(1)}, s32[64]{0:T(128)}, u32[]{:S(2)}) copy-start(s32[64]{0:T(128)} %param.10) | copy-start | bytes 772
  10.2 16.2 %copy-start.3 = (s32[64]{0:T(128)S(1)}, s32[64]{0:T(128)}, u32[]{:S(2)}) copy-start(s32[64]{0:T(128)} %param.11) | copy-start | bytes 772
  10.2 20.0 %collective-permute-start.1 = (bf16[1,256,2,256]{3,2,1,0:T(2,128)(2,1)S(1)}, bf16[1,256,2,256]{3,2,1,0:T(2,128)(2,1)S(1)}, u32[]{:S(2)}, u32[]{:S(2)}) collective-permute-start(bf16[1,256,2,256]{3,2,1,0:T(2,128)(2,1)S(1)} %copy-done.1), channel_id=1, source_target_pairs={{0,8},{2,10},{4,12},{6,14},{8,0},{10,2},{12,4},{14,6},{1,9},{3,11}... | collective-permute-start | bytes 786440 | tf_op jit(solution)/shard_map/ppermute | solution.py:127
  26.4 3.8 %collective-permute-start = (bf16[16,16,512]{2,1,0:T(8,128)(2,1)S(1)}, bf16[16,16,512]{2,1,0:T(8,128)(2,1)S(1)}, u32[]{:S(2)}, u32[]{:S(2)}) collective-permute-start(bf16[16,16,512]{2,1,0:T(8,128)(2,1)S(1)} %all-to-all-done), channel_id=1, source_target_pairs={{0,1},{1,0},{2,3},{3,2},{4,5},{5,4},{6,7},{7,6},{8,9},{9,8},{10,11... | collective-permute-start | bytes 786440 | tf_op jit(solution)/shard_map/ppermute | solution.py:130
  39.4 8.7 %copy-start = (bf16[1,128,2048]{2,1,0:T(8,128)(2,1)S(1)}, bf16[1,128,2048]{2,1,0:T(8,128)(2,1)}, u32[]{:S(2)}) copy-start(bf16[1,128,2048]{2,1,0:T(8,128)(2,1)} %param.6) | copy-start | bytes 1572868

commit v4 on v3

v4 whole, which is shorter than its diff:
```python
import jax
import jax.numpy as jnp
from jax import lax
from jax.experimental import pallas as pl
from jax.experimental.pallas import tpu as pltpu
from jax.sharding import PartitionSpec as P

HD = 128
MEAN = 36
LOG2E = 1.4426950408889634

VMEM_SPEC = pl.BlockSpec(memory_space=pltpu.VMEM)
GRANT = pltpu.CompilerParams(vmem_limit_bytes=16 << 20)
WIDE_GRANT = pltpu.CompilerParams(vmem_limit_bytes=60 << 20)


def normalize(states, norm_gain):
    widened = states.astype(jnp.float32)
    factor = lax.rsqrt(jnp.mean(widened * widened, axis=-1, keepdims=True) + 1e-05)
    return (widened * factor * norm_gain).astype(jnp.bfloat16)


def normalize_kernel(states_ref, gain_ref, out_ref):
    sections, blocks, _, width = out_ref.shape
    depth = width // 2
    normed = normalize(states_ref[...], gain_ref[...])
    for block in range(blocks):
        partner = (block + blocks // 2) % blocks
        for section in range(sections):
            out_ref[section, block, :, :depth] = normed[:, block * depth:(block + 1) * depth]
            out_ref[section, block, :, depth:] = normed[:, partner * depth:(partner + 1) * depth]


def column_blocks(states, norm_gain, sections, blocks):
    rows, width = states.shape
    depth = width // blocks
    shape = (sections, blocks, rows, 2 * depth)
    if depth % HD == 0 and rows % 16 == 0:
        out = pl.pallas_call(
            normalize_kernel,
            out_shape=jax.ShapeDtypeStruct(shape, jnp.bfloat16),
            in_specs=[VMEM_SPEC] * 2,
            out_specs=VMEM_SPEC,
            compiler_params=WIDE_GRANT,
            name="normalize",
        )(states, norm_gain[None, :])
    else:
        columns = normalize(states, norm_gain).reshape(rows, blocks, depth).transpose(1, 0, 2)
        columns = jnp.concatenate([columns, jnp.roll(columns, -(blocks // 2), axis=0)], axis=2)
        out = jnp.broadcast_to(columns[None], shape)
    return out.reshape(-1, rows, 2 * depth)


def live_positions(span_len, span_owner, blocks, sections, cores, rows, core):
    index = lax.iota(jnp.int32, sections * blocks * rows)
    row = index % rows
    block = index // rows % blocks
    section = index // (rows * blocks)
    within = (section * cores + core) * rows + row
    owner = span_owner[:, None]
    length = span_len[:, None]
    load = jnp.sum(jnp.where(owner == block[None, :], length, 0), axis=0)
    before = jnp.sum(jnp.where(owner < block[None, :], length, 0), axis=0)
    return jnp.where(within < load, before + within, -1)[None, :]


def project_kernel(
    own_position_ref,
    other_position_ref,
    own_rows_ref,
    other_rows_ref,
    own_weight_ref,
    other_weight_ref,
    key_ref,
    value_ref,
    key_part_ref,
    value_part_ref,
):
    depth = own_weight_ref.shape[0]
    slots, width = key_ref.shape
    own_rows = own_rows_ref[...]
    wanted = lax.broadcasted_iota(jnp.int32, (slots, own_rows.shape[0]), 0)
    own_pick = jnp.where(wanted == own_position_ref[...], 1.0, 0.0).astype(jnp.bfloat16)
    other_pick = jnp.where(wanted == other_position_ref[...], 1.0, 0.0).astype(jnp.bfloat16)
    picked = jnp.dot(own_pick, own_rows, preferred_element_type=jnp.float32)
    picked += jnp.dot(other_pick, other_rows_ref[...], preferred_element_type=jnp.float32)
    picked = picked.astype(jnp.bfloat16)
    projected = jnp.dot(picked[:, :depth], own_weight_ref[...], preferred_element_type=jnp.float32)
    projected += jnp.dot(picked[:, depth:], other_weight_ref[...], preferred_element_type=jnp.float32)
    key_ref[...] = projected[:, :width]
    value_ref[...] = projected[:, width:]
    key_part_ref[...] = projected[:, :width].astype(jnp.bfloat16)
    value_part_ref[...] = projected[:, width:].astype(jnp.bfloat16)


def add_kernel(own_ref, received_ref, sum_ref, part_ref):
    total = own_ref[...] + received_ref[...].astype(jnp.float32)
    sum_ref[...] = total
    part_ref[...] = total.astype(jnp.bfloat16)


def add(own, received):
    return pl.pallas_call(
        add_kernel,
        out_shape=(
            jax.ShapeDtypeStruct(own.shape, jnp.float32),
            jax.ShapeDtypeStruct(own.shape, jnp.bfloat16),
        ),
        in_specs=[VMEM_SPEC] * 2,
        out_specs=(VMEM_SPEC,) * 2,
        compiler_params=GRANT,
        name="add",
    )(own, received)


def attend_kernel(query_ref, key_ref, key_part_ref, value_ref, value_part_ref, out_ref):
    heads = query_ref.shape[1] // HD
    count = query_ref.shape[0]
    keys = (key_ref[...] + key_part_ref[...].astype(jnp.float32)).astype(jnp.bfloat16)
    values = (value_ref[...] + value_part_ref[...].astype(jnp.float32)).astype(jnp.bfloat16)
    stacked = jnp.concatenate([query_ref[:, head * HD:(head + 1) * HD] for head in range(heads)], axis=0)
    scores = lax.dot_general(stacked, keys, (((1,), (1,)), ((), ())), preferred_element_type=jnp.float32)
    peak = jnp.max(scores, axis=-1, keepdims=True)
    weights = jnp.exp2((scores - peak) * (LOG2E * HD ** -0.5))
    denominator = jnp.sum(weights, axis=-1, keepdims=True)
    numerator = jnp.dot(weights.astype(jnp.bfloat16), values, preferred_element_type=jnp.float32)
    attended = (numerator * (1.0 / denominator)).astype(jnp.bfloat16)
    for head in range(heads):
        out_ref[:, head * HD:(head + 1) * HD] = attended[head * count:(head + 1) * count]


def local(queries, encoder_states, norm_gain, kv_weight, span_len, span_owner):
    sections, blocks, cores = (lax.axis_size(name) for name in ("section", "blk", "mp"))
    rows, features = encoder_states.shape
    depth = features // blocks
    local_groups = kv_weight.shape[3] // HD
    half = blocks // 2
    slots = MEAN * blocks
    query_rows, query_width = queries.shape[1:]
    core = lax.axis_index("mp")

    other_weight = lax.ppermute(kv_weight, "blk", [(b, (b + half) % blocks) for b in range(blocks)])
    outgoing = column_blocks(encoder_states, norm_gain, sections, blocks)
    own_rows = lax.all_to_all(outgoing, ("section", "blk"), 0, 0, tiled=True)
    other_rows = lax.ppermute(own_rows, "mp", [(c, (c + 1) % cores) for c in range(cores)])

    own_position = live_positions(span_len, span_owner, blocks, sections, cores, rows, core)
    other_position = live_positions(span_len, span_owner, blocks, sections, cores, rows, cores - 1 - core)
    width = kv_weight.shape[3]
    keys, values, key_part, value_part = pl.pallas_call(
        project_kernel,
        out_shape=(jax.ShapeDtypeStruct((slots, width), jnp.float32),) * 2
        + (jax.ShapeDtypeStruct((slots, width), jnp.bfloat16),) * 2,
        in_specs=[VMEM_SPEC] * 6,
        out_specs=(VMEM_SPEC,) * 4,
        compiler_params=GRANT,
        name="project",
    )(
        own_position,
        other_position,
        own_rows.reshape(-1, 2 * depth),
        other_rows.reshape(-1, 2 * depth),
        kv_weight[0].reshape(depth, -1),
        other_weight[0].reshape(depth, -1),
    )

    bits = [1 << place for place in range((half - 1).bit_length())]
    for step, (key_bit, value_bit) in enumerate(zip(bits, bits[1:] + bits[:1])):
        if step > 0:
            keys, key_part = add(keys, key_part)
            values, value_part = add(values, value_part)
        key_part = lax.ppermute(key_part, "blk", [(b, b ^ key_bit) for b in range(blocks)])
        value_part = lax.ppermute(value_part, "blk", [(b, b ^ value_bit) for b in range(blocks)])

    group_width = query_width // local_groups
    query_spec = pl.BlockSpec((query_rows, group_width), lambda g: (0, g))
    slot_spec = pl.BlockSpec((slots, HD), lambda g: (0, g))
    attended = pl.pallas_call(
        attend_kernel,
        grid=(local_groups,),
        out_shape=jax.ShapeDtypeStruct((query_rows, query_width), jnp.bfloat16),
        in_specs=[query_spec] + [slot_spec] * 4,
        out_specs=query_spec,
        compiler_params=GRANT,
        name="attend",
    )(queries[0], keys, key_part, values, value_part)
    return attended[None]


def solution(mesh):
    in_specs = (
        P("section", "blk", "mp"),
        P(("blk", "section", "mp"), None),
        P(),
        P("section", "blk", None, "mp"),
        P(),
        P(),
    )
    out_specs = P("section", "blk", "mp")
    return jax.shard_map(local, mesh=mesh, in_specs=in_specs, out_specs=out_specs, check_vma=False)
```

time: 50.6 us -> 46 us (0.909)
  blocking collectives: 17.4 us -> 0 us
  waiting for transfers between devices: 16.9 us -> 27.9 us
  starting transfers between devices: 11.4 us -> 13 us
    all_to_all x2 -> x0, blocking collectives: 17.4 us -> none  [the longest x1 8.7 us: local(): lax.all_to_all(partial, 'blk', 0, 0, tiled=True, axis_index_groups=halves)]
    ppermute x0 -> x4, waiting for transfers between devices: none -> 11 us  [the longest x2 6.46 us: local(): lax.ppermute(key_part, 'blk', [(b, b ^ key_bit) for b in range(blocks)])]
    ppermute x0 -> x4, starting transfers between devices: none -> 1.67 us  [the longest x2 1.6 us: local(): lax.ppermute(key_part, 'blk', [(b, b ^ key_bit) for b in range(blocks)])]
  transfers between devices with their start and end apart: 3 -> 7, of which waited for: 2 -> 6; matrix products, arithmetic and copies ran while one was open for 0% -> 0% of each run, Pallas kernels for 0% -> 0%
where the time goes in v4:
time: 46 us; the launch traced here: 45.8 us
  waiting for transfers between devices  27.9 us (61%)
  starting transfers between devices  13 us (28%)
  Pallas kernels  4.49 us (10%)
    all_to_all x1, waiting for transfers between devices, local(): own_rows = lax.all_to_all(outgoing, ('section', 'blk'), 0, 0, tiled=True)  13.3 us
    all_to_all x1, starting transfers between devices, local(): own_rows = lax.all_to_all(outgoing, ('section', 'blk'), 0, 0, tiled=True)  8.47 us
    ppermute x2, waiting for transfers between devices, local(): lax.ppermute(key_part, 'blk', [(b, b ^ key_bit) for b in range(blocks)])  6.46 us
    ppermute x2, waiting for transfers between devices, local(): lax.ppermute(value_part, 'blk', [(b, b ^ value_bit) for b in range(blocks)])  4.56 us
    ppermute x1, waiting for transfers between devices, local(): lax.ppermute(kv_weight, 'blk', [(b, (b + half) % blocks) for b in range(b...  3.62 us
    ppermute x1, starting transfers between devices, local(): lax.ppermute(kv_weight, 'blk', [(b, (b + half) % blocks) for b in range(b...  2.89 us
    pallas_call x1, Pallas kernels, local(): pl.pallas_call(attend_kernel, grid=(local_groups,), out_shape=jax.ShapeDt...  2.2 us
    pallas_call x1, Pallas kernels, column_blocks(): pl.pallas_call(normalize_kernel, out_shape=jax.ShapeDtypeStruct(shape, jn...  1.67 us
  transfers between devices with their start and end apart: 7, of which 6 were waited for; matrix products, arithmetic and copies ran while one was open for 0% of the time, Pallas kernels for 0%

profile of v4, /device:TPU:0, one launch (start us, length us, event | category | flops | bytes accessed | tf_op | source)
XLA Modules:
  0.0 45.8 jit_solution(1713915267560206668)
XLA Ops:
  0.0 1.7 %normalize.1 = bf16[2,8,16,512]{3,2,1,0:T(8,128)(2,1)} custom-call(bf16[16,2048]{1,0:T(8,128)(2,1)} %states_ref.1, f32[1,2048]{1,0:T(1,128)} %bitcast.22), custom_call_target="tpu_custom_call" | custom-call | tf_op jit(solution)/shard_map/normalize/pallas_call | solution.py:39
  1.7 0.0 copy-start.1
  1.7 8.5 %all-to-all-start = ((bf16[16,16,512]{2,1,0:T(8,128)(2,1)}), bf16[16,16,512]{2,1,0:T(8,128)(2,1)S(1)}, u32[]{:S(2)}, u32[]{:S(2)}) async-start(bf16[16,16,512]{2,1,0:T(8,128)(2,1)} %bitcast.19), calls=%async_computation | async-start | bytes 524288 | tf_op jit(solution)/shard_map/all_to_all | solution.py:144
  10.2 0.0 copy-done.1
  10.2 0.0 copy-start.2
  10.2 0.0 copy-start.3
  10.2 2.9 %collective-permute-start.1 = (bf16[1,256,2,256]{3,2,1,0:T(2,128)(2,1)S(1)}, bf16[1,256,2,256]{3,2,1,0:T(2,128)(2,1)S(1)}, u32[]{:S(2)}, u32[]{:S(2)}) collective-permute-start(bf16[1,256,2,256]{3,2,1,0:T(2,128)(2,1)S(1)} %copy-done.1), channel_id=1, source_target_pairs={{0,8},{2,10},{4,12},{6,14},{8,0},{10,2},{12,4},{14,6},{1,9},{3,11}... | collective-permute-start | bytes 786440 | tf_op jit(solution)/shard_map/ppermute | solution.py:142
  13.1 13.3 %all-to-all-done = bf16[16,16,512]{2,1,0:T(8,128)(2,1)S(1)} async-done(((bf16[16,16,512]{2,1,0:T(8,128)(2,1)}), bf16[16,16,512]{2,1,0:T(8,128)(2,1)S(1)}, u32[]{:S(2)}, u32[]{:S(2)}) %all-to-all-start) | async-done | bytes 262176 | tf_op jit(solution)/shard_map/all_to_all | solution.py:144
  26.4 0.0 collective-permute-start
  26.4 0.0 copy-done.2
  26.4 0.0 copy-done.3
  26.4 0.1 select_reduce_fusion
  26.5 3.6 %collective-permute-done.1 = bf16[1,256,2,256]{3,2,1,0:T(2,128)(2,1)S(1)} collective-permute-done((bf16[1,256,2,256]{3,2,1,0:T(2,128)(2,1)S(1)}, bf16[1,256,2,256]{3,2,1,0:T(2,128)(2,1)S(1)}, u32[]{:S(2)}, u32[]{:S(2)}) %collective-permute-start.1) | collective-permute-done | bytes 262176 | tf_op jit(solution)/shard_map/ppermute | solution.py:142
  30.2 0.0 collective-permute-done
  30.2 0.5 %project.1 = (f32[288,256]{1,0:T(8,128)S(1)}, f32[288,256]{1,0:T(8,128)S(1)}, bf16[288,256]{1,0:T(8,128)(2,1)S(1)}, bf16[288,256]{1,0:T(8,128)(2,1)S(1)}) custom-call(s32[1,256]{1,0:T(1,128)S(1)} %get-tuple-element.24.own_position_ref, s32[1,256]{1,0:T(1,128)S(1)} %get-tuple-element.23.other_position_ref, bf16[256,512]{1,0:T(8,128)(2,1)S(1)} %bitcast.14, ...), custom_call_target="tpu_custom_call" | custom-call | tf_op jit(solution)/shard_map/project/pallas_call | solution.py:150
  30.8 0.0 copy-start
  30.8 1.5 %collective-permute-start.2 = (bf16[288,256]{1,0:T(8,128)(2,1)S(1)}, bf16[288,256]{1,0:T(8,128)(2,1)S(1)}, u32[]{:S(2)}, u32[]{:S(2)}) collective-permute-start(bf16[288,256]{1,0:T(8,128)(2,1)S(1)} %get-tuple-element.14), channel_id=1, source_target_pairs={{0,2},{2,0},{4,6},{6,4},{8,10},{10,8},{12,14},{14,12},{1,3},{3,1},... | collective-permute-start | bytes 442376 | tf_op jit(solution)/shard_map/ppermute | solution.py:172
  32.3 0.0 collective-permute-start.4
  32.3 3.7 %collective-permute-done.2.received_ref = bf16[288,256]{1,0:T(8,128)(2,1)S(1)} collective-permute-done((bf16[288,256]{1,0:T(8,128)(2,1)S(1)}, bf16[288,256]{1,0:T(8,128)(2,1)S(1)}, u32[]{:S(2)}, u32[]{:S(2)}) %collective-permute-start.2) | collective-permute-done | bytes 147488 | tf_op jit(solution)/shard_map/ppermute | solution.py:172
  36.0 0.1 collective-permute-start.3
  36.1 2.2 %collective-permute-done.4.received_ref = bf16[288,256]{1,0:T(8,128)(2,1)S(1)} collective-permute-done((bf16[288,256]{1,0:T(8,128)(2,1)S(1)}, bf16[288,256]{1,0:T(8,128)(2,1)S(1)}, u32[]{:S(2)}, u32[]{:S(2)}) %collective-permute-start.4) | collective-permute-done | bytes 147488 | tf_op jit(solution)/shard_map/ppermute | solution.py:173
  38.4 0.1 collective-permute-start.5
  38.4 2.8 %collective-permute-done.3.key_part_ref = bf16[288,256]{1,0:T(8,128)(2,1)S(1)} collective-permute-done((bf16[288,256]{1,0:T(8,128)(2,1)S(1)}, bf16[288,256]{1,0:T(8,128)(2,1)S(1)}, u32[]{:S(2)}, u32[]{:S(2)}) %collective-permute-start.3) | collective-permute-done | bytes 147488 | tf_op jit(solution)/shard_map/ppermute | solution.py:172
  41.2 2.3 %collective-permute-done.5.value_part_ref = bf16[288,256]{1,0:T(8,128)(2,1)S(1)} collective-permute-done((bf16[288,256]{1,0:T(8,128)(2,1)S(1)}, bf16[288,256]{1,0:T(8,128)(2,1)S(1)}, u32[]{:S(2)}, u32[]{:S(2)}) %collective-permute-start.5) | collective-permute-done | bytes 147488 | tf_op jit(solution)/shard_map/ppermute | solution.py:173
  43.6 0.0 copy-done
  43.6 2.2 %attend.1 = bf16[128,2048]{1,0:T(8,128)(2,1)} custom-call(bf16[128,2048]{1,0:T(8,128)(2,1)S(1)} %bitcast.17, f32[288,256]{1,0:T(8,128)S(1)} %get-tuple-element.15.key_ref, bf16[288,256]{1,0:T(8,128)(2,1)S(1)} %collective-permute-done.3.key_part_ref, f32[288,256]{1,0:T(8,128)S(1)} %get-tuple-element.19.value_ref, ...), custom_call_target="tpu_custom_call" | custom-call | tf_op jit(solution)/shard_map/attend/pallas_call | solution.py:178
  (6 shorter events, 0.2 us)
Async XLA Ops:
  1.7 8.5 %copy-start.1 = (bf16[1,256,2,256]{3,2,1,0:T(2,128)(2,1)S(1)}, bf16[1,256,2,256]{3,2,1,0:T(2,128)(2,1)}, u32[]{:S(2)}) copy-start(bf16[1,256,2,256]{3,2,1,0:T(2,128)(2,1)} %param.9) | copy-start | bytes 786436
  1.7 24.7 %all-to-all-start = ((bf16[16,16,512]{2,1,0:T(8,128)(2,1)}), bf16[16,16,512]{2,1,0:T(8,128)(2,1)S(1)}, u32[]{:S(2)}, u32[]{:S(2)}) async-start(bf16[16,16,512]{2,1,0:T(8,128)(2,1)} %bitcast.19), calls=%async_computation | async-start | bytes 524288 | tf_op jit(solution)/shard_map/all_to_all | solution.py:144
  10.2 16.2 %copy-start.2 = (s32[64]{0:T(128)S(1)}, s32[64]{0:T(128)}, u32[]{:S(2)}) copy-start(s32[64]{0:T(128)} %param.10) | copy-start | bytes 772
  10.2 16.2 %copy-start.3 = (s32[64]{0:T(128)S(1)}, s32[64]{0:T(128)}, u32[]{:S(2)}) copy-start(s32[64]{0:T(128)} %param.11) | copy-start | bytes 772
  10.2 20.0 %collective-permute-start.1 = (bf16[1,256,2,256]{3,2,1,0:T(2,128)(2,1)S(1)}, bf16[1,256,2,256]{3,2,1,0:T(2,128)(2,1)S(1)}, u32[]{:S(2)}, u32[]{:S(2)}) collective-permute-start(bf16[1,256,2,256]{3,2,1,0:T(2,128)(2,1)S(1)} %copy-done.1), channel_id=1, source_target_pairs={{0,8},{2,10},{4,12},{6,14},{8,0},{10,2},{12,4},{14,6},{1,9},{3,11}... | collective-permute-start | bytes 786440 | tf_op jit(solution)/shard_map/ppermute | solution.py:142
  26.4 3.8 %collective-permute-start = (bf16[16,16,512]{2,1,0:T(8,128)(2,1)S(1)}, bf16[16,16,512]{2,1,0:T(8,128)(2,1)S(1)}, u32[]{:S(2)}, u32[]{:S(2)}) collective-permute-start(bf16[16,16,512]{2,1,0:T(8,128)(2,1)S(1)} %all-to-all-done), channel_id=1, source_target_pairs={{0,1},{1,0},{2,3},{3,2},{4,5},{5,4},{6,7},{7,6},{8,9},{9,8},{10,11... | collective-permute-start | bytes 786440 | tf_op jit(solution)/shard_map/ppermute | solution.py:145
  30.8 12.8 %copy-start = (bf16[1,128,2048]{2,1,0:T(8,128)(2,1)S(1)}, bf16[1,128,2048]{2,1,0:T(8,128)(2,1)}, u32[]{:S(2)}) copy-start(bf16[1,128,2048]{2,1,0:T(8,128)(2,1)} %param.6) | copy-start | bytes 1572868
  30.8 5.2 %collective-permute-start.2 = (bf16[288,256]{1,0:T(8,128)(2,1)S(1)}, bf16[288,256]{1,0:T(8,128)(2,1)S(1)}, u32[]{:S(2)}, u32[]{:S(2)}) collective-permute-start(bf16[288,256]{1,0:T(8,128)(2,1)S(1)} %get-tuple-element.14), channel_id=1, source_target_pairs={{0,2},{2,0},{4,6},{6,4},{8,10},{10,8},{12,14},{14,12},{1,3},{3,1},... | collective-permute-start | bytes 442376 | tf_op jit(solution)/shard_map/ppermute | solution.py:172
  32.3 6.0 %collective-permute-start.4 = (bf16[288,256]{1,0:T(8,128)(2,1)S(1)}, bf16[288,256]{1,0:T(8,128)(2,1)S(1)}, u32[]{:S(2)}, u32[]{:S(2)}) collective-permute-start(bf16[288,256]{1,0:T(8,128)(2,1)S(1)} %get-tuple-element.18), channel_id=1, source_target_pairs={{0,4},{2,6},{4,0},{6,2},{8,12},{10,14},{12,8},{14,10},{1,5},{3,7},... | collective-permute-start | bytes 442376 | tf_op jit(solution)/shard_map/ppermute | solution.py:173
  36.0 5.2 %collective-permute-start.3 = (bf16[288,256]{1,0:T(8,128)(2,1)S(1)}, bf16[288,256]{1,0:T(8,128)(2,1)S(1)}, u32[]{:S(2)}, u32[]{:S(2)}) collective-permute-start(bf16[288,256]{1,0:T(8,128)(2,1)S(1)} %get-tuple-element.16), channel_id=1, source_target_pairs={{0,4},{2,6},{4,0},{6,2},{8,12},{10,14},{12,8},{14,10},{1,5},{3,7},... | collective-permute-start | bytes 442376 | tf_op jit(solution)/shard_map/ppermute | solution.py:172
  38.4 5.2 %collective-permute-start.5 = (bf16[288,256]{1,0:T(8,128)(2,1)S(1)}, bf16[288,256]{1,0:T(8,128)(2,1)S(1)}, u32[]{:S(2)}, u32[]{:S(2)}) collective-permute-start(bf16[288,256]{1,0:T(8,128)(2,1)S(1)} %get-tuple-element.20), channel_id=1, source_target_pairs={{0,2},{2,0},{4,6},{6,4},{8,10},{10,8},{12,14},{14,12},{1,3},{3,1},... | collective-permute-start | bytes 442376 | tf_op jit(solution)/shard_map/ppermute | solution.py:173

commit v5 on v4

--- a/solution.py
+++ b/solution.py
@@ -1,3 +1,5 @@
+import functools
+
 import jax
 import jax.numpy as jnp
 from jax import lax
@@ -9,6 +11,7 @@
 MEAN = 36
 LOG2E = 1.4426950408889634
 
+ANY_SPEC = pl.BlockSpec(memory_space=pl.ANY)
 VMEM_SPEC = pl.BlockSpec(memory_space=pltpu.VMEM)
 GRANT = pltpu.CompilerParams(vmem_limit_bytes=16 << 20)
 WIDE_GRANT = pltpu.CompilerParams(vmem_limit_bytes=60 << 20)
@@ -71,13 +74,11 @@
     other_rows_ref,
     own_weight_ref,
     other_weight_ref,
-    key_ref,
-    value_ref,
-    key_part_ref,
-    value_part_ref,
+    *out_refs,
 ):
     depth = own_weight_ref.shape[0]
-    slots, width = key_ref.shape
+    groups = len(out_refs) // 2
+    slots = out_refs[0].shape[0]
     own_rows = own_rows_ref[...]
     wanted = lax.broadcasted_iota(jnp.int32, (slots, own_rows.shape[0]), 0)
     own_pick = jnp.where(wanted == own_position_ref[...], 1.0, 0.0).astype(jnp.bfloat16)
@@ -87,10 +88,13 @@
     picked = picked.astype(jnp.bfloat16)
     projected = jnp.dot(picked[:, :depth], own_weight_ref[...], preferred_element_type=jnp.float32)
     projected += jnp.dot(picked[:, depth:], other_weight_ref[...], preferred_element_type=jnp.float32)
-    key_ref[...] = projected[:, :width]
-    value_ref[...] = projected[:, width:]
-    key_part_ref[...] = projected[:, :width].astype(jnp.bfloat16)
-    value_part_ref[...] = projected[:, width:].astype(jnp.bfloat16)
+    for group in range(groups):
+        sum_ref, part_ref = out_refs[group], out_refs[groups + group]
+        for kind in range(2):
+            tile = kind * groups + group
+            columns = projected[:, tile * HD:(tile + 1) * HD]
+            sum_ref[:, kind * HD:(kind + 1) * HD] = columns
+            part_ref[:, kind * HD:(kind + 1) * HD] = columns.astype(jnp.bfloat16)
 
 
 def add_kernel(own_ref, received_ref, sum_ref, part_ref):
@@ -113,20 +117,41 @@
     )(own, received)
 
 
-def attend_kernel(query_ref, key_ref, key_part_ref, value_ref, value_part_ref, out_ref):
-    heads = query_ref.shape[1] // HD
+def attend(group, heads, query_ref, sum_ref, part_ref, out_ref):
     count = query_ref.shape[0]
-    keys = (key_ref[...] + key_part_ref[...].astype(jnp.float32)).astype(jnp.bfloat16)
-    values = (value_ref[...] + value_part_ref[...].astype(jnp.float32)).astype(jnp.bfloat16)
-    stacked = jnp.concatenate([query_ref[:, head * HD:(head + 1) * HD] for head in range(heads)], axis=0)
-    scores = lax.dot_general(stacked, keys, (((1,), (1,)), ((), ())), preferred_element_type=jnp.float32)
+    first = group * heads
+    total = (sum_ref[...] + part_ref[...].astype(jnp.float32)).astype(jnp.bfloat16)
+    stacked = jnp.concatenate(
+        [query_ref[:, head * HD:(head + 1) * HD] for head in range(first, first + heads)], axis=0
+    )
+    scores = lax.dot_general(stacked, total[:, :HD], (((1,), (1,)), ((), ())), preferred_element_type=jnp.float32)
     peak = jnp.max(scores, axis=-1, keepdims=True)
     weights = jnp.exp2((scores - peak) * (LOG2E * HD ** -0.5))
     denominator = jnp.sum(weights, axis=-1, keepdims=True)
-    numerator = jnp.dot(weights.astype(jnp.bfloat16), values, preferred_element_type=jnp.float32)
+    numerator = jnp.dot(weights.astype(jnp.bfloat16), total[:, HD:], preferred_element_type=jnp.float32)
     attended = (numerator * (1.0 / denominator)).astype(jnp.bfloat16)
     for head in range(heads):
         out_ref[:, head * HD:(head + 1) * HD] = attended[head * count:(head + 1) * count]
+
+
+def attend_kernel(group, query_ref, sum_ref, part_ref, out_ref):
+    attend(group, out_ref.shape[1] // HD, query_ref, sum_ref, part_ref, out_ref)
+
+
+def last_attend_kernel(query_ref, sum_ref, part_ref, *rest):
+    earlier, out_ref, stage, sem = rest[:-3], rest[-3], rest[-2], rest[-1]
+    width = stage.shape[1]
+    sources = (*earlier, stage)
+    copies = [
+        pltpu.make_async_copy(source, out_ref.at[:, group * width:(group + 1) * width], sem.at[group])
+        for group, source in enumerate(sources)
+    ]
+    for copy in copies[:-1]:
+        copy.start()
+    attend(len(earlier), width // HD, query_ref, sum_ref, part_ref, stage)
+    copies[-1].start()
+    for copy in copies:
+        copy.wait()
 
 
 def local(queries, encoder_states, norm_gain, kv_weight, span_len, span_owner):
@@ -146,13 +171,12 @@
 
     own_position = live_positions(span_len, span_owner, blocks, sections, cores, rows, core)
     other_position = live_positions(span_len, span_owner, blocks, sections, cores, rows, cores - 1 - core)
-    width = kv_weight.shape[3]
-    keys, values, key_part, value_part = pl.pallas_call(
+    outputs = pl.pallas_call(
         project_kernel,
-        out_shape=(jax.ShapeDtypeStruct((slots, width), jnp.float32),) * 2
-        + (jax.ShapeDtypeStruct((slots, width), jnp.bfloat16),) * 2,
+        out_shape=(jax.ShapeDtypeStruct((slots, 2 * HD), jnp.float32),) * local_groups
+        + (jax.ShapeDtypeStruct((slots, 2 * HD), jnp.bfloat16),) * local_groups,
         in_specs=[VMEM_SPEC] * 6,
-        out_specs=(VMEM_SPEC,) * 4,
+        out_specs=(VMEM_SPEC,) * (2 * local_groups),
         compiler_params=GRANT,
         name="project",
     )(
@@ -164,26 +188,36 @@
         other_weight[0].reshape(depth, -1),
     )
 
+    sums, parts = list(outputs[:local_groups]), list(outputs[local_groups:])
     bits = [1 << place for place in range((half - 1).bit_length())]
-    for step, (key_bit, value_bit) in enumerate(zip(bits, bits[1:] + bits[:1])):
-        if step > 0:
-            keys, key_part = add(keys, key_part)
-            values, value_part = add(values, value_part)
-        key_part = lax.ppermute(key_part, "blk", [(b, b ^ key_bit) for b in range(blocks)])
-        value_part = lax.ppermute(value_part, "blk", [(b, b ^ value_bit) for b in range(blocks)])
-
-    group_width = query_width // local_groups
-    query_spec = pl.BlockSpec((query_rows, group_width), lambda g: (0, g))
-    slot_spec = pl.BlockSpec((slots, HD), lambda g: (0, g))
+    for step in range(len(bits)):
+        for group in range(local_groups):
+            if step > 0:
+                sums[group], parts[group] = add(sums[group], parts[group])
+            bit = bits[(step + group) % len(bits)]
+            parts[group] = lax.ppermute(parts[group], "blk", [(b, b ^ bit) for b in range(blocks)])
+
+    group_shape = (query_rows, query_width // local_groups)
+    attended = [
+        pl.pallas_call(
+            functools.partial(attend_kernel, group),
+            out_shape=jax.ShapeDtypeStruct(group_shape, jnp.bfloat16),
+            in_specs=[VMEM_SPEC] * 3,
+            out_specs=VMEM_SPEC,
+            compiler_params=GRANT,
+            name="attend",
+        )(queries[0], sums[group], parts[group])
+        for group in range(local_groups - 1)
+    ]
     attended = pl.pallas_call(
-        attend_kernel,
-        grid=(local_groups,),
+        last_attend_kernel,
         out_shape=jax.ShapeDtypeStruct((query_rows, query_width), jnp.bfloat16),
-        in_specs=[query_spec] + [slot_spec] * 4,
-        out_specs=query_spec,
+        in_specs=[VMEM_SPEC] * (2 + local_groups),
+        out_specs=ANY_SPEC,
+        scratch_shapes=[pltpu.VMEM(group_shape, jnp.bfloat16), pltpu.SemaphoreType.DMA((local_groups,))],
         compiler_params=GRANT,
-        name="attend",
-    )(queries[0], keys, key_part, values, value_part)
+        name="attend_last",
+    )(queries[0], sums[-1], parts[-1], *attended)
     return attended[None]
 
 

time: 46 us -> 45.2 us (0.983)
  waiting for transfers between devices: 27.9 us -> 27.3 us
    ppermute x4, waiting for transfers between devices: 11 us -> 10.4 us  [local(): lax.ppermute(parts[group], 'blk', [(b, b ^ bit) for b in range(blocks)])]
    pallas_call x2 -> x3, Pallas kernels: 2.75 us -> 2.58 us  [the longest x1 1.38 us: local(): pl.pallas_call(last_attend_kernel, out_shape=jax.ShapeDtypeStruct((query_...]
  transfers between devices with their start and end apart: 7 -> 7, of which waited for: 6 -> 6; matrix products, arithmetic and copies ran while one was open for 0% -> 0% of each run, Pallas kernels for 0% -> 2%
where the time goes in v5:
time: 45.2 us; the launch traced here: 44.9 us
  waiting for transfers between devices  27.3 us (60%)
  starting transfers between devices  13 us (29%)
  Pallas kernels  4.33 us (10%)
    all_to_all x1, waiting for transfers between devices, local(): own_rows = lax.all_to_all(outgoing, ('section', 'blk'), 0, 0, tiled=True)  13.3 us
    ppermute x4, waiting for transfers between devices, local(): lax.ppermute(parts[group], 'blk', [(b, b ^ bit) for b in range(blocks)])  10.4 us
    all_to_all x1, starting transfers between devices, local(): own_rows = lax.all_to_all(outgoing, ('section', 'blk'), 0, 0, tiled=True)  8.47 us
    ppermute x1, waiting for transfers between devices, local(): lax.ppermute(kv_weight, 'blk', [(b, (b + half) % blocks) for b in range(b...  3.62 us
    ppermute x1, starting transfers between devices, local(): lax.ppermute(kv_weight, 'blk', [(b, (b + half) % blocks) for b in range(b...  2.89 us
    ppermute x4, starting transfers between devices, local(): lax.ppermute(parts[group], 'blk', [(b, b ^ bit) for b in range(blocks)])  1.67 us
    pallas_call x1, Pallas kernels, column_blocks(): pl.pallas_call(normalize_kernel, out_shape=jax.ShapeDtypeStruct(shape, jn...  1.67 us
    pallas_call x1, Pallas kernels, local(): pl.pallas_call(last_attend_kernel, out_shape=jax.ShapeDtypeStruct((query_...  1.38 us
  transfers between devices with their start and end apart: 7, of which 6 were waited for; matrix products, arithmetic and copies ran while one was open for 0% of the time, Pallas kernels for 2%

profile of v5, /device:TPU:0, one launch (start us, length us, event | category | flops | bytes accessed | tf_op | source)
XLA Modules:
  0.0 44.9 jit_solution(13394268579848352095)
XLA Ops:
  0.0 1.7 %normalize.1 = bf16[2,8,16,512]{3,2,1,0:T(8,128)(2,1)} custom-call(bf16[16,2048]{1,0:T(8,128)(2,1)} %states_ref.1, f32[1,2048]{1,0:T(1,128)} %bitcast.23), custom_call_target="tpu_custom_call" | custom-call | tf_op jit(solution)/shard_map/normalize/pallas_call | solution.py:42
  1.7 0.0 copy-start.1
  1.7 8.5 %all-to-all-start = ((bf16[16,16,512]{2,1,0:T(8,128)(2,1)}), bf16[16,16,512]{2,1,0:T(8,128)(2,1)S(1)}, u32[]{:S(2)}, u32[]{:S(2)}) async-start(bf16[16,16,512]{2,1,0:T(8,128)(2,1)} %bitcast.20), calls=%async_computation | async-start | bytes 524288 | tf_op jit(solution)/shard_map/all_to_all | solution.py:169
  10.2 0.0 copy-done.1
  10.2 0.0 copy-start.2
  10.2 0.0 copy-start.3
  10.2 2.9 %collective-permute-start.1 = (bf16[1,256,2,256]{3,2,1,0:T(2,128)(2,1)S(1)}, bf16[1,256,2,256]{3,2,1,0:T(2,128)(2,1)S(1)}, u32[]{:S(2)}, u32[]{:S(2)}) collective-permute-start(bf16[1,256,2,256]{3,2,1,0:T(2,128)(2,1)S(1)} %copy-done.1), channel_id=1, source_target_pairs={{0,8},{2,10},{4,12},{6,14},{8,0},{10,2},{12,4},{14,6},{1,9},{3,11}... | collective-permute-start | bytes 786440 | tf_op jit(solution)/shard_map/ppermute | solution.py:167
  13.1 13.3 %all-to-all-done = bf16[16,16,512]{2,1,0:T(8,128)(2,1)S(1)} async-done(((bf16[16,16,512]{2,1,0:T(8,128)(2,1)}), bf16[16,16,512]{2,1,0:T(8,128)(2,1)S(1)}, u32[]{:S(2)}, u32[]{:S(2)}) %all-to-all-start) | async-done | bytes 262176 | tf_op jit(solution)/shard_map/all_to_all | solution.py:169
  26.4 0.0 collective-permute-start
  26.4 0.0 copy-done.2
  26.4 0.0 copy-done.3
  26.4 0.1 select_reduce_fusion
  26.5 3.6 %collective-permute-done.1 = bf16[1,256,2,256]{3,2,1,0:T(2,128)(2,1)S(1)} collective-permute-done((bf16[1,256,2,256]{3,2,1,0:T(2,128)(2,1)S(1)}, bf16[1,256,2,256]{3,2,1,0:T(2,128)(2,1)S(1)}, u32[]{:S(2)}, u32[]{:S(2)}) %collective-permute-start.1) | collective-permute-done | bytes 262176 | tf_op jit(solution)/shard_map/ppermute | solution.py:167
  30.2 0.0 collective-permute-done
  30.2 0.5 %project.1 = (f32[288,256]{1,0:T(8,128)S(1)}, f32[288,256]{1,0:T(8,128)S(1)}, bf16[288,256]{1,0:T(8,128)(2,1)S(1)}, bf16[288,256]{1,0:T(8,128)(2,1)S(1)}) custom-call(s32[1,256]{1,0:T(1,128)S(1)} %get-tuple-element.24.own_position_ref, s32[1,256]{1,0:T(1,128)S(1)} %get-tuple-element.23.other_position_ref, bf16[256,512]{1,0:T(8,128)(2,1)S(1)} %bitcast.16, ...), custom_call_target="tpu_custom_call" | custom-call | tf_op jit(solution)/shard_map/project/pallas_call | solution.py:174
  30.8 0.0 copy-start
  30.8 1.5 %collective-permute-start.4 = (bf16[288,256]{1,0:T(8,128)(2,1)S(1)}, bf16[288,256]{1,0:T(8,128)(2,1)S(1)}, u32[]{:S(2)}, u32[]{:S(2)}) collective-permute-start(bf16[288,256]{1,0:T(8,128)(2,1)S(1)} %get-tuple-element.18), channel_id=1, source_target_pairs={{0,2},{2,0},{4,6},{6,4},{8,10},{10,8},{12,14},{14,12},{1,3},{3,1},... | collective-permute-start | bytes 442376 | tf_op jit(solution)/shard_map/ppermute | solution.py:198
  32.3 0.0 collective-permute-start.2
  32.3 3.7 %collective-permute-done.4.received_ref = bf16[288,256]{1,0:T(8,128)(2,1)S(1)} collective-permute-done((bf16[288,256]{1,0:T(8,128)(2,1)S(1)}, bf16[288,256]{1,0:T(8,128)(2,1)S(1)}, u32[]{:S(2)}, u32[]{:S(2)}) %collective-permute-start.4) | collective-permute-done | bytes 147488 | tf_op jit(solution)/shard_map/ppermute | solution.py:198
  36.0 0.1 collective-permute-start.5
  36.1 2.2 %collective-permute-done.2.received_ref = bf16[288,256]{1,0:T(8,128)(2,1)S(1)} collective-permute-done((bf16[288,256]{1,0:T(8,128)(2,1)S(1)}, bf16[288,256]{1,0:T(8,128)(2,1)S(1)}, u32[]{:S(2)}, u32[]{:S(2)}) %collective-permute-start.2) | collective-permute-done | bytes 147488 | tf_op jit(solution)/shard_map/ppermute | solution.py:198
  38.4 0.1 collective-permute-start.3
  38.4 2.8 %collective-permute-done.5.part_ref = bf16[288,256]{1,0:T(8,128)(2,1)S(1)} collective-permute-done((bf16[288,256]{1,0:T(8,128)(2,1)S(1)}, bf16[288,256]{1,0:T(8,128)(2,1)S(1)}, u32[]{:S(2)}, u32[]{:S(2)}) %collective-permute-start.5) | collective-permute-done | bytes 147488 | tf_op jit(solution)/shard_map/ppermute | solution.py:198
  41.2 0.0 copy-done
  41.2 0.7 %attend.1.rest_0_ = bf16[128,1024]{1,0:T(8,128)(2,1)S(1)} custom-call(bf16[128,2048]{1,0:T(8,128)(2,1)S(1)} %bitcast.14, f32[288,256]{1,0:T(8,128)S(1)} %get-tuple-element.19.sum_ref, bf16[288,256]{1,0:T(8,128)(2,1)S(1)} %collective-permute-done.5.part_ref), custom_call_target="tpu_custom_call" | custom-call | tf_op jit(solution)/shard_map/attend/pallas_call | solution.py:202
  41.9 1.7 %collective-permute-done.3.part_ref = bf16[288,256]{1,0:T(8,128)(2,1)S(1)} collective-permute-done((bf16[288,256]{1,0:T(8,128)(2,1)S(1)}, bf16[288,256]{1,0:T(8,128)(2,1)S(1)}, u32[]{:S(2)}, u32[]{:S(2)}) %collective-permute-start.3) | collective-permute-done | bytes 147488 | tf_op jit(solution)/shard_map/ppermute | solution.py:198
  43.6 1.4 %attend_last.1 = bf16[128,2048]{1,0:T(8,128)(2,1)} custom-call(bf16[128,2048]{1,0:T(8,128)(2,1)S(1)} %bitcast.15, f32[288,256]{1,0:T(8,128)S(1)} %get-tuple-element.15.sum_ref, bf16[288,256]{1,0:T(8,128)(2,1)S(1)} %collective-permute-done.3.part_ref, bf16[128,1024]{1,0:T(8,128)(2,1)S(1)} %attend.1.rest_0_), custom_call_target="tpu_custom_call" | custom-call | tf_op jit(solution)/shard_map/attend_last/pallas_call | solution.py:212
  (6 shorter events, 0.2 us)
Async XLA Ops:
  1.7 8.5 %copy-start.1 = (bf16[1,256,2,256]{3,2,1,0:T(2,128)(2,1)S(1)}, bf16[1,256,2,256]{3,2,1,0:T(2,128)(2,1)}, u32[]{:S(2)}) copy-start(bf16[1,256,2,256]{3,2,1,0:T(2,128)(2,1)} %param.9) | copy-start | bytes 786436
  1.7 24.7 %all-to-all-start = ((bf16[16,16,512]{2,1,0:T(8,128)(2,1)}), bf16[16,16,512]{2,1,0:T(8,128)(2,1)S(1)}, u32[]{:S(2)}, u32[]{:S(2)}) async-start(bf16[16,16,512]{2,1,0:T(8,128)(2,1)} %bitcast.20), calls=%async_computation | async-start | bytes 524288 | tf_op jit(solution)/shard_map/all_to_all | solution.py:169
  10.2 16.2 %copy-start.2 = (s32[64]{0:T(128)S(1)}, s32[64]{0:T(128)}, u32[]{:S(2)}) copy-start(s32[64]{0:T(128)} %param.10) | copy-start | bytes 772
  10.2 16.2 %copy-start.3 = (s32[64]{0:T(128)S(1)}, s32[64]{0:T(128)}, u32[]{:S(2)}) copy-start(s32[64]{0:T(128)} %param.11) | copy-start | bytes 772
  10.2 20.0 %collective-permute-start.1 = (bf16[1,256,2,256]{3,2,1,0:T(2,128)(2,1)S(1)}, bf16[1,256,2,256]{3,2,1,0:T(2,128)(2,1)S(1)}, u32[]{:S(2)}, u32[]{:S(2)}) collective-permute-start(bf16[1,256,2,256]{3,2,1,0:T(2,128)(2,1)S(1)} %copy-done.1), channel_id=1, source_target_pairs={{0,8},{2,10},{4,12},{6,14},{8,0},{10,2},{12,4},{14,6},{1,9},{3,11}... | collective-permute-start | bytes 786440 | tf_op jit(solution)/shard_map/ppermute | solution.py:167
  26.4 3.8 %collective-permute-start = (bf16[16,16,512]{2,1,0:T(8,128)(2,1)S(1)}, bf16[16,16,512]{2,1,0:T(8,128)(2,1)S(1)}, u32[]{:S(2)}, u32[]{:S(2)}) collective-permute-start(bf16[16,16,512]{2,1,0:T(8,128)(2,1)S(1)} %all-to-all-done), channel_id=1, source_target_pairs={{0,1},{1,0},{2,3},{3,2},{4,5},{5,4},{6,7},{7,6},{8,9},{9,8},{10,11... | collective-permute-start | bytes 786440 | tf_op jit(solution)/shard_map/ppermute | solution.py:170
  30.8 10.5 %copy-start = (bf16[1,128,2048]{2,1,0:T(8,128)(2,1)S(1)}, bf16[1,128,2048]{2,1,0:T(8,128)(2,1)}, u32[]{:S(2)}) copy-start(bf16[1,128,2048]{2,1,0:T(8,128)(2,1)} %param.6) | copy-start | bytes 1572868
  30.8 5.2 %collective-permute-start.4 = (bf16[288,256]{1,0:T(8,128)(2,1)S(1)}, bf16[288,256]{1,0:T(8,128)(2,1)S(1)}, u32[]{:S(2)}, u32[]{:S(2)}) collective-permute-start(bf16[288,256]{1,0:T(8,128)(2,1)S(1)} %get-tuple-element.18), channel_id=1, source_target_pairs={{0,2},{2,0},{4,6},{6,4},{8,10},{10,8},{12,14},{14,12},{1,3},{3,1},... | collective-permute-start | bytes 442376 | tf_op jit(solution)/shard_map/ppermute | solution.py:198
  32.3 6.0 %collective-permute-start.2 = (bf16[288,256]{1,0:T(8,128)(2,1)S(1)}, bf16[288,256]{1,0:T(8,128)(2,1)S(1)}, u32[]{:S(2)}, u32[]{:S(2)}) collective-permute-start(bf16[288,256]{1,0:T(8,128)(2,1)S(1)} %get-tuple-element.14), channel_id=1, source_target_pairs={{0,4},{2,6},{4,0},{6,2},{8,12},{10,14},{12,8},{14,10},{1,5},{3,7},... | collective-permute-start | bytes 442376 | tf_op jit(solution)/shard_map/ppermute | solution.py:198
  36.0 5.2 %collective-permute-start.5 = (bf16[288,256]{1,0:T(8,128)(2,1)S(1)}, bf16[288,256]{1,0:T(8,128)(2,1)S(1)}, u32[]{:S(2)}, u32[]{:S(2)}) collective-permute-start(bf16[288,256]{1,0:T(8,128)(2,1)S(1)} %get-tuple-element.20), channel_id=1, source_target_pairs={{0,4},{2,6},{4,0},{6,2},{8,12},{10,14},{12,8},{14,10},{1,5},{3,7},... | collective-permute-start | bytes 442376 | tf_op jit(solution)/shard_map/ppermute | solution.py:198
  38.4 5.2 %collective-permute-start.3 = (bf16[288,256]{1,0:T(8,128)(2,1)S(1)}, bf16[288,256]{1,0:T(8,128)(2,1)S(1)}, u32[]{:S(2)}, u32[]{:S(2)}) collective-permute-start(bf16[288,256]{1,0:T(8,128)(2,1)S(1)} %get-tuple-element.16), channel_id=1, source_target_pairs={{0,2},{2,0},{4,6},{6,4},{8,10},{10,8},{12,14},{14,12},{1,3},{3,1},... | collective-permute-start | bytes 442376 | tf_op jit(solution)/shard_map/ppermute | solution.py:198

commit v6 on v5

--- a/solution.py
+++ b/solution.py
@@ -92,15 +92,27 @@
         sum_ref, part_ref = out_refs[group], out_refs[groups + group]
         for kind in range(2):
             tile = kind * groups + group
-            columns = projected[:, tile * HD:(tile + 1) * HD]
-            sum_ref[:, kind * HD:(kind + 1) * HD] = columns
-            part_ref[:, kind * HD:(kind + 1) * HD] = columns.astype(jnp.bfloat16)
+            sum_ref[:, kind * HD:(kind + 1) * HD] = projected[:, tile * HD:(tile + 1) * HD]
+        pack(sum_ref[...], part_ref)
+
+
+def pack(total, part_ref):
+    keys = total[:, :HD]
+    high = keys.astype(jnp.bfloat16)
+    part_ref[:, :HD] = high
+    part_ref[:, HD:2 * HD] = (keys - high.astype(jnp.float32)).astype(jnp.bfloat16)
+    part_ref[:, 2 * HD:] = total[:, HD:].astype(jnp.bfloat16)
+
+
+def summed(own_ref, received_ref):
+    high, rest, values = (received_ref[:, k * HD:(k + 1) * HD].astype(jnp.float32) for k in range(3))
+    return jnp.concatenate([own_ref[:, :HD] + (high + rest), own_ref[:, HD:] + values], axis=1)
 
 
 def add_kernel(own_ref, received_ref, sum_ref, part_ref):
-    total = own_ref[...] + received_ref[...].astype(jnp.float32)
+    total = summed(own_ref, received_ref)
     sum_ref[...] = total
-    part_ref[...] = total.astype(jnp.bfloat16)
+    pack(total, part_ref)
 
 
 def add(own, received):
@@ -108,7 +120,7 @@
         add_kernel,
         out_shape=(
             jax.ShapeDtypeStruct(own.shape, jnp.float32),
-            jax.ShapeDtypeStruct(own.shape, jnp.bfloat16),
+            jax.ShapeDtypeStruct(received.shape, jnp.bfloat16),
         ),
         in_specs=[VMEM_SPEC] * 2,
         out_specs=(VMEM_SPEC,) * 2,
@@ -120,7 +132,7 @@
 def attend(group, heads, query_ref, sum_ref, part_ref, out_ref):
     count = query_ref.shape[0]
     first = group * heads
-    total = (sum_ref[...] + part_ref[...].astype(jnp.float32)).astype(jnp.bfloat16)
+    total = summed(sum_ref, part_ref).astype(jnp.bfloat16)
     stacked = jnp.concatenate(
         [query_ref[:, head * HD:(head + 1) * HD] for head in range(first, first + heads)], axis=0
     )
@@ -174,7 +186,7 @@
     outputs = pl.pallas_call(
         project_kernel,
         out_shape=(jax.ShapeDtypeStruct((slots, 2 * HD), jnp.float32),) * local_groups
-        + (jax.ShapeDtypeStruct((slots, 2 * HD), jnp.bfloat16),) * local_groups,
+        + (jax.ShapeDtypeStruct((slots, 3 * HD), jnp.bfloat16),) * local_groups,
         in_specs=[VMEM_SPEC] * 6,
         out_specs=(VMEM_SPEC,) * (2 * local_groups),
         compiler_params=GRANT,

time: 45.2 us -> 46.4 us (1.027)
  waiting for transfers between devices: 27.3 us -> 28.1 us
    ppermute x4, waiting for transfers between devices: 10.4 us -> 11.2 us  [local(): lax.ppermute(parts[group], 'blk', [(b, b ^ bit) for b in range(blocks)])]
where the time goes in v6:
time: 46.4 us; the launch traced here: 46.1 us
  waiting for transfers between devices  28.1 us (61%)
  starting transfers between devices  13.3 us (29%)
  Pallas kernels  4.42 us (10%)
    all_to_all x1, waiting for transfers between devices, local(): own_rows = lax.all_to_all(outgoing, ('section', 'blk'), 0, 0, tiled=True)  13.3 us
    ppermute x4, waiting for transfers between devices, local(): lax.ppermute(parts[group], 'blk', [(b, b ^ bit) for b in range(blocks)])  11.2 us
    all_to_all x1, starting transfers between devices, local(): own_rows = lax.all_to_all(outgoing, ('section', 'blk'), 0, 0, tiled=True)  8.47 us
    ppermute x1, waiting for transfers between devices, local(): lax.ppermute(kv_weight, 'blk', [(b, (b + half) % blocks) for b in range(b...  3.62 us
    ppermute x1, starting transfers between devices, local(): lax.ppermute(kv_weight, 'blk', [(b, (b + half) % blocks) for b in range(b...  2.89 us
    ppermute x4, starting transfers between devices, local(): lax.ppermute(parts[group], 'blk', [(b, b ^ bit) for b in range(blocks)])  1.96 us
    pallas_call x1, Pallas kernels, column_blocks(): pl.pallas_call(normalize_kernel, out_shape=jax.ShapeDtypeStruct(shape, jn...  1.67 us
    pallas_call x1, Pallas kernels, local(): pl.pallas_call(last_attend_kernel, out_shape=jax.ShapeDtypeStruct((query_...  1.39 us
  transfers between devices with their start and end apart: 7, of which 6 were waited for; matrix products, arithmetic and copies ran while one was open for 0% of the time, Pallas kernels for 2%

profile of v6, /device:TPU:0, one launch (start us, length us, event | category | flops | bytes accessed | tf_op | source)
XLA Modules:
  0.0 46.1 jit_solution(5920690282463107358)
XLA Ops:
  0.0 1.7 %normalize.1 = bf16[2,8,16,512]{3,2,1,0:T(8,128)(2,1)} custom-call(bf16[16,2048]{1,0:T(8,128)(2,1)} %states_ref.1, f32[1,2048]{1,0:T(1,128)} %bitcast.23), custom_call_target="tpu_custom_call" | custom-call | tf_op jit(solution)/shard_map/normalize/pallas_call | solution.py:42
  1.7 0.0 copy-start.1
  1.7 8.5 %all-to-all-start = ((bf16[16,16,512]{2,1,0:T(8,128)(2,1)}), bf16[16,16,512]{2,1,0:T(8,128)(2,1)S(1)}, u32[]{:S(2)}, u32[]{:S(2)}) async-start(bf16[16,16,512]{2,1,0:T(8,128)(2,1)} %bitcast.20), calls=%async_computation | async-start | bytes 524288 | tf_op jit(solution)/shard_map/all_to_all | solution.py:181
  10.2 0.0 copy-done.1
  10.2 0.0 copy-start.2
  10.2 0.0 copy-start.3
  10.2 2.9 %collective-permute-start.1 = (bf16[1,256,2,256]{3,2,1,0:T(2,128)(2,1)S(1)}, bf16[1,256,2,256]{3,2,1,0:T(2,128)(2,1)S(1)}, u32[]{:S(2)}, u32[]{:S(2)}) collective-permute-start(bf16[1,256,2,256]{3,2,1,0:T(2,128)(2,1)S(1)} %copy-done.1), channel_id=1, source_target_pairs={{0,8},{2,10},{4,12},{6,14},{8,0},{10,2},{12,4},{14,6},{1,9},{3,11}... | collective-permute-start | bytes 786440 | tf_op jit(solution)/shard_map/ppermute | solution.py:179
  13.1 13.3 %all-to-all-done = bf16[16,16,512]{2,1,0:T(8,128)(2,1)S(1)} async-done(((bf16[16,16,512]{2,1,0:T(8,128)(2,1)}), bf16[16,16,512]{2,1,0:T(8,128)(2,1)S(1)}, u32[]{:S(2)}, u32[]{:S(2)}) %all-to-all-start) | async-done | bytes 262176 | tf_op jit(solution)/shard_map/all_to_all | solution.py:181
  26.4 0.0 collective-permute-start
  26.4 0.0 copy-done.2
  26.4 0.0 copy-done.3
  26.4 0.1 select_reduce_fusion
  26.5 3.6 %collective-permute-done.1 = bf16[1,256,2,256]{3,2,1,0:T(2,128)(2,1)S(1)} collective-permute-done((bf16[1,256,2,256]{3,2,1,0:T(2,128)(2,1)S(1)}, bf16[1,256,2,256]{3,2,1,0:T(2,128)(2,1)S(1)}, u32[]{:S(2)}, u32[]{:S(2)}) %collective-permute-start.1) | collective-permute-done | bytes 262176 | tf_op jit(solution)/shard_map/ppermute | solution.py:179
  30.2 0.0 collective-permute-done
  30.2 0.6 %project.1 = (f32[288,256]{1,0:T(8,128)S(1)}, f32[288,256]{1,0:T(8,128)S(1)}, bf16[288,384]{1,0:T(8,128)(2,1)S(1)}, bf16[288,384]{1,0:T(8,128)(2,1)S(1)}) custom-call(s32[1,256]{1,0:T(1,128)S(1)} %get-tuple-element.24.own_position_ref, s32[1,256]{1,0:T(1,128)S(1)} %get-tuple-element.23.other_position_ref, bf16[256,512]{1,0:T(8,128)(2,1)S(1)} %bitcast.16, ...), custom_call_target="tpu_custom_call" | custom-call | tf_op jit(solution)/shard_map/project/pallas_call | solution.py:186
  30.8 0.0 copy-start
  30.8 1.5 %collective-permute-start.4 = (bf16[288,384]{1,0:T(8,128)(2,1)S(1)}, bf16[288,384]{1,0:T(8,128)(2,1)S(1)}, u32[]{:S(2)}, u32[]{:S(2)}) collective-permute-start(bf16[288,384]{1,0:T(8,128)(2,1)S(1)} %get-tuple-element.18), channel_id=1, source_target_pairs={{0,2},{2,0},{4,6},{6,4},{8,10},{10,8},{12,14},{14,12},{1,3},{3,1},... | collective-permute-start | bytes 663560 | tf_op jit(solution)/shard_map/ppermute | solution.py:210
  32.3 0.0 collective-permute-start.2
  32.3 4.9 %collective-permute-done.4.received_ref = bf16[288,384]{1,0:T(8,128)(2,1)S(1)} collective-permute-done((bf16[288,384]{1,0:T(8,128)(2,1)S(1)}, bf16[288,384]{1,0:T(8,128)(2,1)S(1)}, u32[]{:S(2)}, u32[]{:S(2)}) %collective-permute-start.4) | collective-permute-done | bytes 221216 | tf_op jit(solution)/shard_map/ppermute | solution.py:210
  37.2 0.1 add.143
  37.3 0.1 collective-permute-start.5
  37.4 1.3 %collective-permute-done.2.received_ref = bf16[288,384]{1,0:T(8,128)(2,1)S(1)} collective-permute-done((bf16[288,384]{1,0:T(8,128)(2,1)S(1)}, bf16[288,384]{1,0:T(8,128)(2,1)S(1)}, u32[]{:S(2)}, u32[]{:S(2)}) %collective-permute-start.2) | collective-permute-done | bytes 221216 | tf_op jit(solution)/shard_map/ppermute | solution.py:210
  38.7 0.1 add.142
  38.7 0.4 collective-permute-start.3
  39.1 4.2 %collective-permute-done.5.part_ref = bf16[288,384]{1,0:T(8,128)(2,1)S(1)} collective-permute-done((bf16[288,384]{1,0:T(8,128)(2,1)S(1)}, bf16[288,384]{1,0:T(8,128)(2,1)S(1)}, u32[]{:S(2)}, u32[]{:S(2)}) %collective-permute-start.5) | collective-permute-done | bytes 221216 | tf_op jit(solution)/shard_map/ppermute | solution.py:210
  43.3 0.0 copy-done
  43.3 0.7 %attend.1.rest_0_ = bf16[128,1024]{1,0:T(8,128)(2,1)S(1)} custom-call(bf16[128,2048]{1,0:T(8,128)(2,1)S(1)} %bitcast.14, f32[288,256]{1,0:T(8,128)S(1)} %get-tuple-element.19.sum_ref, bf16[288,384]{1,0:T(8,128)(2,1)S(1)} %collective-permute-done.5.part_ref), custom_call_target="tpu_custom_call" | custom-call | tf_op jit(solution)/shard_map/attend/pallas_call | solution.py:214
  44.0 0.8 %collective-permute-done.3.part_ref = bf16[288,384]{1,0:T(8,128)(2,1)S(1)} collective-permute-done((bf16[288,384]{1,0:T(8,128)(2,1)S(1)}, bf16[288,384]{1,0:T(8,128)(2,1)S(1)}, u32[]{:S(2)}, u32[]{:S(2)}) %collective-permute-start.3) | collective-permute-done | bytes 221216 | tf_op jit(solution)/shard_map/ppermute | solution.py:210
  44.7 1.4 %attend_last.1 = bf16[128,2048]{1,0:T(8,128)(2,1)} custom-call(bf16[128,2048]{1,0:T(8,128)(2,1)S(1)} %bitcast.15, f32[288,256]{1,0:T(8,128)S(1)} %get-tuple-element.15.sum_ref, bf16[288,384]{1,0:T(8,128)(2,1)S(1)} %collective-permute-done.3.part_ref, bf16[128,1024]{1,0:T(8,128)(2,1)S(1)} %attend.1.rest_0_), custom_call_target="tpu_custom_call" | custom-call | tf_op jit(solution)/shard_map/attend_last/pallas_call | solution.py:224
  (4 shorter events, 0.1 us)
Async XLA Ops:
  1.7 8.5 %copy-start.1 = (bf16[1,256,2,256]{3,2,1,0:T(2,128)(2,1)S(1)}, bf16[1,256,2,256]{3,2,1,0:T(2,128)(2,1)}, u32[]{:S(2)}) copy-start(bf16[1,256,2,256]{3,2,1,0:T(2,128)(2,1)} %param.9) | copy-start | bytes 786436
  1.7 24.7 %all-to-all-start = ((bf16[16,16,512]{2,1,0:T(8,128)(2,1)}), bf16[16,16,512]{2,1,0:T(8,128)(2,1)S(1)}, u32[]{:S(2)}, u32[]{:S(2)}) async-start(bf16[16,16,512]{2,1,0:T(8,128)(2,1)} %bitcast.20), calls=%async_computation | async-start | bytes 524288 | tf_op jit(solution)/shard_map/all_to_all | solution.py:181
  10.2 16.2 %copy-start.2 = (s32[64]{0:T(128)S(1)}, s32[64]{0:T(128)}, u32[]{:S(2)}) copy-start(s32[64]{0:T(128)} %param.10) | copy-start | bytes 772
  10.2 16.2 %copy-start.3 = (s32[64]{0:T(128)S(1)}, s32[64]{0:T(128)}, u32[]{:S(2)}) copy-start(s32[64]{0:T(128)} %param.11) | copy-start | bytes 772
  10.2 20.0 %collective-permute-start.1 = (bf16[1,256,2,256]{3,2,1,0:T(2,128)(2,1)S(1)}, bf16[1,256,2,256]{3,2,1,0:T(2,128)(2,1)S(1)}, u32[]{:S(2)}, u32[]{:S(2)}) collective-permute-start(bf16[1,256,2,256]{3,2,1,0:T(2,128)(2,1)S(1)} %copy-done.1), channel_id=1, source_target_pairs={{0,8},{2,10},{4,12},{6,14},{8,0},{10,2},{12,4},{14,6},{1,9},{3,11}... | collective-permute-start | bytes 786440 | tf_op jit(solution)/shard_map/ppermute | solution.py:179
  26.4 3.8 %collective-permute-start = (bf16[16,16,512]{2,1,0:T(8,128)(2,1)S(1)}, bf16[16,16,512]{2,1,0:T(8,128)(2,1)S(1)}, u32[]{:S(2)}, u32[]{:S(2)}) collective-permute-start(bf16[16,16,512]{2,1,0:T(8,128)(2,1)S(1)} %all-to-all-done), channel_id=1, source_target_pairs={{0,1},{1,0},{2,3},{3,2},{4,5},{5,4},{6,7},{7,6},{8,9},{9,8},{10,11... | collective-permute-start | bytes 786440 | tf_op jit(solution)/shard_map/ppermute | solution.py:182
  30.8 12.5 %copy-start = (bf16[1,128,2048]{2,1,0:T(8,128)(2,1)S(1)}, bf16[1,128,2048]{2,1,0:T(8,128)(2,1)}, u32[]{:S(2)}) copy-start(bf16[1,128,2048]{2,1,0:T(8,128)(2,1)} %param.6) | copy-start | bytes 1572868
  30.8 6.4 %collective-permute-start.4 = (bf16[288,384]{1,0:T(8,128)(2,1)S(1)}, bf16[288,384]{1,0:T(8,128)(2,1)S(1)}, u32[]{:S(2)}, u32[]{:S(2)}) collective-permute-start(bf16[288,384]{1,0:T(8,128)(2,1)S(1)} %get-tuple-element.18), channel_id=1, source_target_pairs={{0,2},{2,0},{4,6},{6,4},{8,10},{10,8},{12,14},{14,12},{1,3},{3,1},... | collective-permute-start | bytes 663560 | tf_op jit(solution)/shard_map/ppermute | solution.py:210
  32.3 6.4 %collective-permute-start.2 = (bf16[288,384]{1,0:T(8,128)(2,1)S(1)}, bf16[288,384]{1,0:T(8,128)(2,1)S(1)}, u32[]{:S(2)}, u32[]{:S(2)}) collective-permute-start(bf16[288,384]{1,0:T(8,128)(2,1)S(1)} %get-tuple-element.14), channel_id=1, source_target_pairs={{0,4},{2,6},{4,0},{6,2},{8,12},{10,14},{12,8},{14,10},{1,5},{3,7},... | collective-permute-start | bytes 663560 | tf_op jit(solution)/shard_map/ppermute | solution.py:210
  37.3 6.0 %collective-permute-start.5 = (bf16[288,384]{1,0:T(8,128)(2,1)S(1)}, bf16[288,384]{1,0:T(8,128)(2,1)S(1)}, u32[]{:S(2)}, u32[]{:S(2)}) collective-permute-start(bf16[288,384]{1,0:T(8,128)(2,1)S(1)} %get-tuple-element.20), channel_id=1, source_target_pairs={{0,4},{2,6},{4,0},{6,2},{8,12},{10,14},{12,8},{14,10},{1,5},{3,7},... | collective-permute-start | bytes 663560 | tf_op jit(solution)/shard_map/ppermute | solution.py:210
  38.7 6.0 %collective-permute-start.3 = (bf16[288,384]{1,0:T(8,128)(2,1)S(1)}, bf16[288,384]{1,0:T(8,128)(2,1)S(1)}, u32[]{:S(2)}, u32[]{:S(2)}) collective-permute-start(bf16[288,384]{1,0:T(8,128)(2,1)S(1)} %get-tuple-element.16), channel_id=1, source_target_pairs={{0,2},{2,0},{4,6},{6,4},{8,10},{10,8},{12,14},{14,12},{1,3},{3,1},... | collective-permute-start | bytes 663560 | tf_op jit(solution)/shard_map/ppermute | solution.py:210

commit v7 on v6

--- a/solution.py
+++ b/solution.py
@@ -77,7 +77,6 @@
     *out_refs,
 ):
     depth = own_weight_ref.shape[0]
-    groups = len(out_refs) // 2
     slots = out_refs[0].shape[0]
     own_rows = own_rows_ref[...]
     wanted = lax.broadcasted_iota(jnp.int32, (slots, own_rows.shape[0]), 0)
@@ -88,25 +87,25 @@
     picked = picked.astype(jnp.bfloat16)
     projected = jnp.dot(picked[:, :depth], own_weight_ref[...], preferred_element_type=jnp.float32)
     projected += jnp.dot(picked[:, depth:], other_weight_ref[...], preferred_element_type=jnp.float32)
-    for group in range(groups):
-        sum_ref, part_ref = out_refs[group], out_refs[groups + group]
-        for kind in range(2):
-            tile = kind * groups + group
-            sum_ref[:, kind * HD:(kind + 1) * HD] = projected[:, tile * HD:(tile + 1) * HD]
-        pack(sum_ref[...], part_ref)
+    chains = len(out_refs) // 2
+    for chain in range(chains):
+        total = projected[:, chain * HD:(chain + 1) * HD]
+        out_refs[chain][...] = total
+        pack(total, out_refs[chains + chain])
 
 
 def pack(total, part_ref):
-    keys = total[:, :HD]
-    high = keys.astype(jnp.bfloat16)
+    high = total.astype(jnp.bfloat16)
     part_ref[:, :HD] = high
-    part_ref[:, HD:2 * HD] = (keys - high.astype(jnp.float32)).astype(jnp.bfloat16)
-    part_ref[:, 2 * HD:] = total[:, HD:].astype(jnp.bfloat16)
+    if part_ref.shape[1] > HD:
+        part_ref[:, HD:] = (total - high.astype(jnp.float32)).astype(jnp.bfloat16)
 
 
 def summed(own_ref, received_ref):
-    high, rest, values = (received_ref[:, k * HD:(k + 1) * HD].astype(jnp.float32) for k in range(3))
-    return jnp.concatenate([own_ref[:, :HD] + (high + rest), own_ref[:, HD:] + values], axis=1)
+    received = received_ref[:, :HD].astype(jnp.float32)
+    if received_ref.shape[1] > HD:
+        received += received_ref[:, HD:].astype(jnp.float32)
+    return own_ref[...] + received
 
 
 def add_kernel(own_ref, received_ref, sum_ref, part_ref):
@@ -129,28 +128,29 @@
     )(own, received)
 
 
-def attend(group, heads, query_ref, sum_ref, part_ref, out_ref):
+def attend(group, heads, query_ref, key_ref, key_part_ref, value_ref, value_part_ref, out_ref):
     count = query_ref.shape[0]
     first = group * heads
-    total = summed(sum_ref, part_ref).astype(jnp.bfloat16)
+    keys = summed(key_ref, key_part_ref).astype(jnp.bfloat16)
+    values = summed(value_ref, value_part_ref).astype(jnp.bfloat16)
     stacked = jnp.concatenate(
         [query_ref[:, head * HD:(head + 1) * HD] for head in range(first, first + heads)], axis=0
     )
-    scores = lax.dot_general(stacked, total[:, :HD], (((1,), (1,)), ((), ())), preferred_element_type=jnp.float32)
+    scores = lax.dot_general(stacked, keys, (((1,), (1,)), ((), ())), preferred_element_type=jnp.float32)
     peak = jnp.max(scores, axis=-1, keepdims=True)
     weights = jnp.exp2((scores - peak) * (LOG2E * HD ** -0.5))
     denominator = jnp.sum(weights, axis=-1, keepdims=True)
-    numerator = jnp.dot(weights.astype(jnp.bfloat16), total[:, HD:], preferred_element_type=jnp.float32)
+    numerator = jnp.dot(weights.astype(jnp.bfloat16), values, preferred_element_type=jnp.float32)
     attended = (numerator * (1.0 / denominator)).astype(jnp.bfloat16)
     for head in range(heads):
         out_ref[:, head * HD:(head + 1) * HD] = attended[head * count:(head + 1) * count]
 
 
-def attend_kernel(group, query_ref, sum_ref, part_ref, out_ref):
-    attend(group, out_ref.shape[1] // HD, query_ref, sum_ref, part_ref, out_ref)
-
-
-def last_attend_kernel(query_ref, sum_ref, part_ref, *rest):
+def attend_kernel(group, query_ref, *refs):
+    attend(group, refs[-1].shape[1] // HD, query_ref, *refs)
+
+
+def last_attend_kernel(query_ref, key_ref, key_part_ref, value_ref, value_part_ref, *rest):
     earlier, out_ref, stage, sem = rest[:-3], rest[-3], rest[-2], rest[-1]
     width = stage.shape[1]
     sources = (*earlier, stage)
@@ -160,7 +160,7 @@
     ]
     for copy in copies[:-1]:
         copy.start()
-    attend(len(earlier), width // HD, query_ref, sum_ref, part_ref, stage)
+    attend(len(earlier), width // HD, query_ref, key_ref, key_part_ref, value_ref, value_part_ref, stage)
     copies[-1].start()
     for copy in copies:
         copy.wait()
@@ -185,10 +185,11 @@
     other_position = live_positions(span_len, span_owner, blocks, sections, cores, rows, cores - 1 - core)
     outputs = pl.pallas_call(
         project_kernel,
-        out_shape=(jax.ShapeDtypeStruct((slots, 2 * HD), jnp.float32),) * local_groups
-        + (jax.ShapeDtypeStruct((slots, 3 * HD), jnp.bfloat16),) * local_groups,
+        out_shape=(jax.ShapeDtypeStruct((slots, HD), jnp.float32),) * (2 * local_groups)
+        + (jax.ShapeDtypeStruct((slots, 2 * HD), jnp.bfloat16),) * local_groups
+        + (jax.ShapeDtypeStruct((slots, HD), jnp.bfloat16),) * local_groups,
         in_specs=[VMEM_SPEC] * 6,
-        out_specs=(VMEM_SPEC,) * (2 * local_groups),
+        out_specs=(VMEM_SPEC,) * (4 * local_groups),
         compiler_params=GRANT,
         name="project",
     )(
@@ -200,36 +201,40 @@
         other_weight[0].reshape(depth, -1),
     )
 
-    sums, parts = list(outputs[:local_groups]), list(outputs[local_groups:])
+    chains = 2 * local_groups
+    sums, parts = list(outputs[:chains]), list(outputs[chains:])
     bits = [1 << place for place in range((half - 1).bit_length())]
     for step in range(len(bits)):
-        for group in range(local_groups):
+        for chain in range(chains):
             if step > 0:
-                sums[group], parts[group] = add(sums[group], parts[group])
-            bit = bits[(step + group) % len(bits)]
-            parts[group] = lax.ppermute(parts[group], "blk", [(b, b ^ bit) for b in range(blocks)])
+                sums[chain], parts[chain] = add(sums[chain], parts[chain])
+            bit = bits[(step + chain) % len(bits)]
+            parts[chain] = lax.ppermute(parts[chain], "blk", [(b, b ^ bit) for b in range(blocks)])
+
+    def summands(group):
+        return [refs[chain] for chain in (group, local_groups + group) for refs in (sums, parts)]
 
     group_shape = (query_rows, query_width // local_groups)
     attended = [
         pl.pallas_call(
             functools.partial(attend_kernel, group),
             out_shape=jax.ShapeDtypeStruct(group_shape, jnp.bfloat16),
-            in_specs=[VMEM_SPEC] * 3,
+            in_specs=[VMEM_SPEC] * 5,
             out_specs=VMEM_SPEC,
             compiler_params=GRANT,
             name="attend",
-        )(queries[0], sums[group], parts[group])
+        )(queries[0], *summands(group))
         for group in range(local_groups - 1)
     ]
     attended = pl.pallas_call(
         last_attend_kernel,
         out_shape=jax.ShapeDtypeStruct((query_rows, query_width), jnp.bfloat16),
-        in_specs=[VMEM_SPEC] * (2 + local_groups),
+        in_specs=[VMEM_SPEC] * (4 + local_groups),
         out_specs=ANY_SPEC,
         scratch_shapes=[pltpu.VMEM(group_shape, jnp.bfloat16), pltpu.SemaphoreType.DMA((local_groups,))],
         compiler_params=GRANT,
         name="attend_last",
-    )(queries[0], sums[-1], parts[-1], *attended)
+    )(queries[0], *summands(local_groups - 1), *attended)
     return attended[None]
 
 

time: 46.4 us -> 49.1 us (1.058)
  starting transfers between devices: 13.3 us -> 18.2 us
  waiting for transfers between devices: 28.1 us -> 25.8 us
    ppermute x4 -> x8, starting transfers between devices: 1.96 us -> 6.87 us  [local(): lax.ppermute(parts[chain], 'blk', [(b, b ^ bit) for b in range(blocks)])]
    ppermute x4 -> x8, waiting for transfers between devices: 11.2 us -> 8.93 us  [local(): lax.ppermute(parts[chain], 'blk', [(b, b ^ bit) for b in range(blocks)])]
  transfers between devices with their start and end apart: 7 -> 11, of which waited for: 6 -> 6; matrix products, arithmetic and copies ran while one was open for 0% -> 0% of each run, Pallas kernels for 2% -> 2%
where the time goes in v7:
time: 49.1 us; the launch traced here: 48.8 us
  waiting for transfers between devices  25.8 us (53%)
  starting transfers between devices  18.2 us (37%)
  Pallas kernels  4.41 us (9%)
    all_to_all x1, waiting for transfers between devices, local(): own_rows = lax.all_to_all(outgoing, ('section', 'blk'), 0, 0, tiled=True)  13.3 us
    ppermute x8, waiting for transfers between devices, local(): lax.ppermute(parts[chain], 'blk', [(b, b ^ bit) for b in range(blocks)])  8.93 us
    all_to_all x1, starting transfers between devices, local(): own_rows = lax.all_to_all(outgoing, ('section', 'blk'), 0, 0, tiled=True)  8.47 us
    ppermute x8, starting transfers between devices, local(): lax.ppermute(parts[chain], 'blk', [(b, b ^ bit) for b in range(blocks)])  6.87 us
    ppermute x1, waiting for transfers between devices, local(): lax.ppermute(kv_weight, 'blk', [(b, (b + half) % blocks) for b in range(b...  3.62 us
    ppermute x1, starting transfers between devices, local(): lax.ppermute(kv_weight, 'blk', [(b, (b + half) % blocks) for b in range(b...  2.89 us
    pallas_call x1, Pallas kernels, column_blocks(): pl.pallas_call(normalize_kernel, out_shape=jax.ShapeDtypeStruct(shape, jn...  1.67 us
    pallas_call x1, Pallas kernels, local(): pl.pallas_call(last_attend_kernel, out_shape=jax.ShapeDtypeStruct((query_...  1.39 us
  transfers between devices with their start and end apart: 11, of which 6 were waited for; matrix products, arithmetic and copies ran while one was open for 0% of the time, Pallas kernels for 2%

profile of v7, /device:TPU:0, one launch (start us, length us, event | category | flops | bytes accessed | tf_op | source)
XLA Modules:
  0.0 48.8 jit_solution(6305813417487429217)
XLA Ops:
  0.0 1.7 %normalize.1 = bf16[2,8,16,512]{3,2,1,0:T(8,128)(2,1)} custom-call(bf16[16,2048]{1,0:T(8,128)(2,1)} %states_ref.1, f32[1,2048]{1,0:T(1,128)} %bitcast.23), custom_call_target="tpu_custom_call" | custom-call | tf_op jit(solution)/shard_map/normalize/pallas_call | solution.py:42
  1.7 8.5 %all-to-all-start = ((bf16[16,16,512]{2,1,0:T(8,128)(2,1)}), bf16[16,16,512]{2,1,0:T(8,128)(2,1)S(1)}, u32[]{:S(2)}, u32[]{:S(2)}) async-start(bf16[16,16,512]{2,1,0:T(8,128)(2,1)} %bitcast.20), calls=%async_computation | async-start | bytes 524288 | tf_op jit(solution)/shard_map/all_to_all | solution.py:181
  10.2 0.0 copy-done.1
  10.2 0.0 copy-start.2
  10.2 0.0 copy-start.3
  10.2 2.9 %collective-permute-start.1 = (bf16[1,256,2,256]{3,2,1,0:T(2,128)(2,1)S(1)}, bf16[1,256,2,256]{3,2,1,0:T(2,128)(2,1)S(1)}, u32[]{:S(2)}, u32[]{:S(2)}) collective-permute-start(bf16[1,256,2,256]{3,2,1,0:T(2,128)(2,1)S(1)} %copy-done.1), channel_id=1, source_target_pairs={{0,8},{2,10},{4,12},{6,14},{8,0},{10,2},{12,4},{14,6},{1,9},{3,11}... | collective-permute-start | bytes 786440 | tf_op jit(solution)/shard_map/ppermute | solution.py:179
  13.1 13.3 %all-to-all-done = bf16[16,16,512]{2,1,0:T(8,128)(2,1)S(1)} async-done(((bf16[16,16,512]{2,1,0:T(8,128)(2,1)}), bf16[16,16,512]{2,1,0:T(8,128)(2,1)S(1)}, u32[]{:S(2)}, u32[]{:S(2)}) %all-to-all-start) | async-done | bytes 262176 | tf_op jit(solution)/shard_map/all_to_all | solution.py:181
  26.4 0.0 collective-permute-start
  26.4 0.0 copy-done.2
  26.4 0.0 copy-done.3
  26.4 0.1 select_reduce_fusion
  26.5 3.6 %collective-permute-done.1 = bf16[1,256,2,256]{3,2,1,0:T(2,128)(2,1)S(1)} collective-permute-done((bf16[1,256,2,256]{3,2,1,0:T(2,128)(2,1)S(1)}, bf16[1,256,2,256]{3,2,1,0:T(2,128)(2,1)S(1)}, u32[]{:S(2)}, u32[]{:S(2)}) %collective-permute-start.1) | collective-permute-done | bytes 262176 | tf_op jit(solution)/shard_map/ppermute | solution.py:179
  30.2 0.0 collective-permute-done
  30.2 0.6 %project.1 = (f32[288,128]{1,0:T(8,128)S(1)}, f32[288,128]{1,0:T(8,128)S(1)}, f32[288,128]{1,0:T(8,128)S(1)}, f32[288,128]{1,0:T(8,128)S(1)}, bf16[288,256]{1,0:...) custom-call(s32[1,256]{1,0:T(1,128)S(1)} %get-tuple-element.40.own_posit, ...), custom_call_target="tpu_custom_call" | custom-call | tf_op jit(solution)/shard_map/project/pallas_call | solution.py:186
  30.8 1.5 %collective-permute-start.6 = (bf16[288,256]{1,0:T(8,128)(2,1)S(1)}, bf16[288,256]{1,0:T(8,128)(2,1)S(1)}, u32[]{:S(2)}, u32[]{:S(2)}) collective-permute-start(bf16[288,256]{1,0:T(8,128)(2,1)S(1)} %get-tuple-element.30), channel_id=1, source_target_pairs={{0,2},{2,0},{4,6},{6,4},{8,10},{10,8},{12,14},{14,12},{1,3},{3,1},... | collective-permute-start | bytes 442376 | tf_op jit(solution)/shard_map/ppermute | solution.py:212
  32.3 0.0 collective-permute-start.2
  32.3 0.6 %collective-permute-start.8 = (bf16[288,128]{1,0:T(8,128)(2,1)S(1)}, bf16[288,128]{1,0:T(8,128)(2,1)S(1)}, u32[]{:S(2)}, u32[]{:S(2)}) collective-permute-start(bf16[288,128]{1,0:T(8,128)(2,1)S(1)} %get-tuple-element.34), channel_id=1, source_target_pairs={{0,2},{2,0},{4,6},{6,4},{8,10},{10,8},{12,14},{14,12},{1,3},{3,1},... | collective-permute-start | bytes 221192 | tf_op jit(solution)/shard_map/ppermute | solution.py:212
  32.9 3.5 %collective-permute-done.6.received_ref = bf16[288,256]{1,0:T(8,128)(2,1)S(1)} collective-permute-done((bf16[288,256]{1,0:T(8,128)(2,1)S(1)}, bf16[288,256]{1,0:T(8,128)(2,1)S(1)}, u32[]{:S(2)}, u32[]{:S(2)}) %collective-permute-start.6) | collective-permute-done | bytes 147488 | tf_op jit(solution)/shard_map/ppermute | solution.py:212
  36.5 0.1 collective-permute-start.7
  36.5 2.0 %collective-permute-start.4 = (bf16[288,128]{1,0:T(8,128)(2,1)S(1)}, bf16[288,128]{1,0:T(8,128)(2,1)S(1)}, u32[]{:S(2)}, u32[]{:S(2)}) collective-permute-start(bf16[288,128]{1,0:T(8,128)(2,1)S(1)} %get-tuple-element.26), channel_id=1, source_target_pairs={{0,4},{2,6},{4,0},{6,2},{8,12},{10,14},{12,8},{14,10},{1,5},{3,7},... | collective-permute-start | bytes 221192 | tf_op jit(solution)/shard_map/ppermute | solution.py:212
  38.5 0.0 collective-permute-done.2.received_ref
  38.6 1.5 %collective-permute-start.3 = (bf16[288,256]{1,0:T(8,128)(2,1)S(1)}, bf16[288,256]{1,0:T(8,128)(2,1)S(1)}, u32[]{:S(2)}, u32[]{:S(2)}) collective-permute-start(bf16[288,256]{1,0:T(8,128)(2,1)S(1)} %get-tuple-element.24), channel_id=1, source_target_pairs={{0,2},{2,0},{4,6},{6,4},{8,10},{10,8},{12,14},{14,12},{1,3},{3,1},... | collective-permute-start | bytes 442376 | tf_op jit(solution)/shard_map/ppermute | solution.py:212
  40.1 0.0 collective-permute-done.8.received_ref
  40.2 0.1 collective-permute-start.9
  40.3 2.7 %collective-permute-done.4.received_ref = bf16[288,128]{1,0:T(8,128)(2,1)S(1)} collective-permute-done((bf16[288,128]{1,0:T(8,128)(2,1)S(1)}, bf16[288,128]{1,0:T(8,128)(2,1)S(1)}, u32[]{:S(2)}, u32[]{:S(2)}) %collective-permute-start.4) | collective-permute-done | bytes 73760 | tf_op jit(solution)/shard_map/ppermute | solution.py:212
  43.0 1.0 %collective-permute-start.5 = (bf16[288,128]{1,0:T(8,128)(2,1)S(1)}, bf16[288,128]{1,0:T(8,128)(2,1)S(1)}, u32[]{:S(2)}, u32[]{:S(2)}) collective-permute-start(bf16[288,128]{1,0:T(8,128)(2,1)S(1)} %get-tuple-element.28), channel_id=1, source_target_pairs={{0,2},{2,0},{4,6},{6,4},{8,10},{10,8},{12,14},{14,12},{1,3},{3,1},... | collective-permute-start | bytes 221192 | tf_op jit(solution)/shard_map/ppermute | solution.py:212
  44.0 0.6 %collective-permute-done.9.refs_3_ = bf16[288,128]{1,0:T(8,128)(2,1)S(1)} collective-permute-done((bf16[288,128]{1,0:T(8,128)(2,1)S(1)}, bf16[288,128]{1,0:T(8,128)(2,1)S(1)}, u32[]{:S(2)}, u32[]{:S(2)}) %collective-permute-start.9) | collective-permute-done | bytes 73760 | tf_op jit(solution)/shard_map/ppermute | solution.py:212
  44.6 0.0 collective-permute-done.7.refs_1_
  44.6 0.7 %attend.1.rest_0_ = bf16[128,1024]{1,0:T(8,128)(2,1)S(1)} custom-call(bf16[128,2048]{1,0:T(8,128)(2,1)S(1)} %bitcast.14, f32[288,128]{1,0:T(8,128)S(1)} %get-tuple-element.31.refs_0_, bf16[288,256]{1,0:T(8,128)(2,1)S(1)} %collective-permute-done.7.refs_1_, f32[288,128]{1,0:T(8,128)S(1)} %get-tuple-element.35.refs_2_, ...), custom_call_target="tpu_custom_call" | custom-call | tf_op jit(solution)/shard_map/attend/pallas_call | solution.py:219
  45.3 2.1 %collective-permute-done.5.value_part_ref = bf16[288,128]{1,0:T(8,128)(2,1)S(1)} collective-permute-done((bf16[288,128]{1,0:T(8,128)(2,1)S(1)}, bf16[288,128]{1,0:T(8,128)(2,1)S(1)}, u32[]{:S(2)}, u32[]{:S(2)}) %collective-permute-start.5) | collective-permute-done | bytes 73760 | tf_op jit(solution)/shard_map/ppermute | solution.py:212
  47.4 0.0 collective-permute-done.3.key_part_ref
  47.4 1.4 %attend_last.1 = bf16[128,2048]{1,0:T(8,128)(2,1)} custom-call(bf16[128,2048]{1,0:T(8,128)(2,1)S(1)} %bitcast.15, f32[288,128]{1,0:T(8,128)S(1)} %get-tuple-element.23.key_ref, bf16[288,256]{1,0:T(8,128)(2,1)S(1)} %collective-permute-done.3.key_part_ref, f32[288,128]{1,0:T(8,128)S(1)} %get-tuple-element.27.value_ref, ...), custom_call_target="tpu_custom_call" | custom-call | tf_op jit(solution)/shard_map/attend_last/pallas_call | solution.py:229
  (11 shorter events, 0.2 us)
Async XLA Ops:
  1.7 8.5 %copy-start.1 = (bf16[1,256,2,256]{3,2,1,0:T(2,128)(2,1)S(1)}, bf16[1,256,2,256]{3,2,1,0:T(2,128)(2,1)}, u32[]{:S(2)}) copy-start(bf16[1,256,2,256]{3,2,1,0:T(2,128)(2,1)} %param.9) | copy-start | bytes 786436
  1.7 24.7 %all-to-all-start = ((bf16[16,16,512]{2,1,0:T(8,128)(2,1)}), bf16[16,16,512]{2,1,0:T(8,128)(2,1)S(1)}, u32[]{:S(2)}, u32[]{:S(2)}) async-start(bf16[16,16,512]{2,1,0:T(8,128)(2,1)} %bitcast.20), calls=%async_computation | async-start | bytes 524288 | tf_op jit(solution)/shard_map/all_to_all | solution.py:181
  10.2 16.2 %copy-start.2 = (s32[64]{0:T(128)S(1)}, s32[64]{0:T(128)}, u32[]{:S(2)}) copy-start(s32[64]{0:T(128)} %param.10) | copy-start | bytes 772
  10.2 16.2 %copy-start.3 = (s32[64]{0:T(128)S(1)}, s32[64]{0:T(128)}, u32[]{:S(2)}) copy-start(s32[64]{0:T(128)} %param.11) | copy-start | bytes 772
  10.2 20.0 %collective-permute-start.1 = (bf16[1,256,2,256]{3,2,1,0:T(2,128)(2,1)S(1)}, bf16[1,256,2,256]{3,2,1,0:T(2,128)(2,1)S(1)}, u32[]{:S(2)}, u32[]{:S(2)}) collective-permute-start(bf16[1,256,2,256]{3,2,1,0:T(2,128)(2,1)S(1)} %copy-done.1), channel_id=1, source_target_pairs={{0,8},{2,10},{4,12},{6,14},{8,0},{10,2},{12,4},{14,6},{1,9},{3,11}... | collective-permute-start | bytes 786440 | tf_op jit(solution)/shard_map/ppermute | solution.py:179
  26.4 3.8 %collective-permute-start = (bf16[16,16,512]{2,1,0:T(8,128)(2,1)S(1)}, bf16[16,16,512]{2,1,0:T(8,128)(2,1)S(1)}, u32[]{:S(2)}, u32[]{:S(2)}) collective-permute-start(bf16[16,16,512]{2,1,0:T(8,128)(2,1)S(1)} %all-to-all-done), channel_id=1, source_target_pairs={{0,1},{1,0},{2,3},{3,2},{4,5},{5,4},{6,7},{7,6},{8,9},{9,8},{10,11... | collective-permute-start | bytes 786440 | tf_op jit(solution)/shard_map/ppermute | solution.py:182
  30.8 5.6 %collective-permute-start.6 = (bf16[288,256]{1,0:T(8,128)(2,1)S(1)}, bf16[288,256]{1,0:T(8,128)(2,1)S(1)}, u32[]{:S(2)}, u32[]{:S(2)}) collective-permute-start(bf16[288,256]{1,0:T(8,128)(2,1)S(1)} %get-tuple-element.30), channel_id=1, source_target_pairs={{0,2},{2,0},{4,6},{6,4},{8,10},{10,8},{12,14},{14,12},{1,3},{3,1},... | collective-permute-start | bytes 442376 | tf_op jit(solution)/shard_map/ppermute | solution.py:212
  32.3 6.3 %collective-permute-start.2 = (bf16[288,256]{1,0:T(8,128)(2,1)S(1)}, bf16[288,256]{1,0:T(8,128)(2,1)S(1)}, u32[]{:S(2)}, u32[]{:S(2)}) collective-permute-start(bf16[288,256]{1,0:T(8,128)(2,1)S(1)} %get-tuple-element.22), channel_id=1, source_target_pairs={{0,4},{2,6},{4,0},{6,2},{8,12},{10,14},{12,8},{14,10},{1,5},{3,7},... | collective-permute-start | bytes 442376 | tf_op jit(solution)/shard_map/ppermute | solution.py:212
  32.3 7.8 %collective-permute-start.8 = (bf16[288,128]{1,0:T(8,128)(2,1)S(1)}, bf16[288,128]{1,0:T(8,128)(2,1)S(1)}, u32[]{:S(2)}, u32[]{:S(2)}) collective-permute-start(bf16[288,128]{1,0:T(8,128)(2,1)S(1)} %get-tuple-element.34), channel_id=1, source_target_pairs={{0,2},{2,0},{4,6},{6,4},{8,10},{10,8},{12,14},{14,12},{1,3},{3,1},... | collective-permute-start | bytes 221192 | tf_op jit(solution)/shard_map/ppermute | solution.py:212
  36.4 8.2 %copy-start = (bf16[1,128,2048]{2,1,0:T(8,128)(2,1)S(1)}, bf16[1,128,2048]{2,1,0:T(8,128)(2,1)}, u32[]{:S(2)}) copy-start(bf16[1,128,2048]{2,1,0:T(8,128)(2,1)} %param.6) | copy-start | bytes 1572868
  36.5 8.1 %collective-permute-start.7 = (bf16[288,256]{1,0:T(8,128)(2,1)S(1)}, bf16[288,256]{1,0:T(8,128)(2,1)S(1)}, u32[]{:S(2)}, u32[]{:S(2)}) collective-permute-start(bf16[288,256]{1,0:T(8,128)(2,1)S(1)} %get-tuple-element.32), channel_id=1, source_target_pairs={{0,4},{2,6},{4,0},{6,2},{8,12},{10,14},{12,8},{14,10},{1,5},{3,7},... | collective-permute-start | bytes 442376 | tf_op jit(solution)/shard_map/ppermute | solution.py:212
  36.5 6.4 %collective-permute-start.4 = (bf16[288,128]{1,0:T(8,128)(2,1)S(1)}, bf16[288,128]{1,0:T(8,128)(2,1)S(1)}, u32[]{:S(2)}, u32[]{:S(2)}) collective-permute-start(bf16[288,128]{1,0:T(8,128)(2,1)S(1)} %get-tuple-element.26), channel_id=1, source_target_pairs={{0,4},{2,6},{4,0},{6,2},{8,12},{10,14},{12,8},{14,10},{1,5},{3,7},... | collective-permute-start | bytes 221192 | tf_op jit(solution)/shard_map/ppermute | solution.py:212
  38.6 8.8 %collective-permute-start.3 = (bf16[288,256]{1,0:T(8,128)(2,1)S(1)}, bf16[288,256]{1,0:T(8,128)(2,1)S(1)}, u32[]{:S(2)}, u32[]{:S(2)}) collective-permute-start(bf16[288,256]{1,0:T(8,128)(2,1)S(1)} %get-tuple-element.24), channel_id=1, source_target_pairs={{0,2},{2,0},{4,6},{6,4},{8,10},{10,8},{12,14},{14,12},{1,3},{3,1},... | collective-permute-start | bytes 442376 | tf_op jit(solution)/shard_map/ppermute | solution.py:212
  40.2 4.4 %collective-permute-start.9 = (bf16[288,128]{1,0:T(8,128)(2,1)S(1)}, bf16[288,128]{1,0:T(8,128)(2,1)S(1)}, u32[]{:S(2)}, u32[]{:S(2)}) collective-permute-start(bf16[288,128]{1,0:T(8,128)(2,1)S(1)} %get-tuple-element.36), channel_id=1, source_target_pairs={{0,4},{2,6},{4,0},{6,2},{8,12},{10,14},{12,8},{14,10},{1,5},{3,7},... | collective-permute-start | bytes 221192 | tf_op jit(solution)/shard_map/ppermute | solution.py:212
  43.0 4.4 %collective-permute-start.5 = (bf16[288,128]{1,0:T(8,128)(2,1)S(1)}, bf16[288,128]{1,0:T(8,128)(2,1)S(1)}, u32[]{:S(2)}, u32[]{:S(2)}) collective-permute-start(bf16[288,128]{1,0:T(8,128)(2,1)S(1)} %get-tuple-element.28), channel_id=1, source_target_pairs={{0,2},{2,0},{4,6},{6,4},{8,10},{10,8},{12,14},{14,12},{1,3},{3,1},... | collective-permute-start | bytes 221192 | tf_op jit(solution)/shard_map/ppermute | solution.py:212
